TPU v7x, 32 devices: a whole 2x2x4 slice. The times are simulated.
32 devices in a mesh: bx: 8 (over z, y), by: 4 (over x, core).
Axes of the slice: x: 2, y: 2, z: 4, core: 2. Of those that a mesh axis runs over, the one named last changes fastest.
Arguments:
- polarization: float32 [3, 8, 256, 512], P(None, None, 'bx', 'by'), may hold values from -1.6 to 1.6
- alpha_field: float32 [8, 256, 512], P(None, 'bx', 'by'), may hold values from -1 to 1
- landau: float32 [3, 8], replicated, may hold values from 0.05 to 0.25
- stiffness: float32 [8], replicated, may hold values from 0.5 to 1.5
- permittivity: float32 [8], replicated, may hold values from 0.5 to 2
- interfaces: float32 [9], replicated, may hold values from 0.0002 to 0.0008
Outputs:
- polar_next: float32 [3, 8, 256, 512], P(None, None, 'bx', 'by')
- depol_field: float32 [3, 8, 256, 512], P(None, None, 'bx', 'by')
All inputs are finite; a program needn't handle non-finite values.
Results may differ from a plain program's by a relative error of at most 0.0003.
Values sent between devices are 32-bit elements; how exact they have to be, the bound alone decides.
A program may use at most 64 MiB of HBM per device.

v0:
```python
import jax
import jax.numpy as jnp
from jax import lax
from jax.sharding import PartitionSpec as P

STEPS = 2


step_size = 0.05
highest = lax.Precision.HIGHEST


def extended(block, sides, width):
    for axis, dim in sides:
        count = lax.axis_size(axis)
        forward = [(i, i + 1) for i in range(count - 1)]
        forward.append((count - 1, 0))
        backward = [(target, source) for source, target in forward]
        low = lax.ppermute(
            lax.slice_in_dim(block, block.shape[dim] - width, None, axis=dim), axis, forward
        )
        high = lax.ppermute(lax.slice_in_dim(block, 0, width, axis=dim), axis, backward)
        block = jnp.concatenate([low, block, high], axis=dim)
    return block


def phase_table(left_index, right_index, length, sign):
    turns = left_index * right_index % length
    angle = 2.0 * jnp.pi / length * turns.astype(jnp.float32)
    return (jnp.cos(angle), sign * jnp.sin(angle))


def mix(form, real_part, imag_part, cos_table, sin_table):
    real_out = jnp.einsum(form, real_part, cos_table, precision=highest) - jnp.einsum(
        form, imag_part, sin_table, precision=highest
    )
    imag_out = jnp.einsum(form, real_part, sin_table, precision=highest) + jnp.einsum(
        form, imag_part, cos_table, precision=highest
    )
    return (real_out, imag_out)


def rotate(real_part, imag_part, cos_table, sin_table):
    return (
        real_part * cos_table - imag_part * sin_table,
        real_part * sin_table + imag_part * cos_table,
    )


def shift_up(source, axis_no):
    upper_part = lax.slice_in_dim(source, 1, source.shape[axis_no], axis=axis_no)
    return jnp.concatenate(
        [upper_part, jnp.zeros_like(lax.slice_in_dim(source, 0, 1, axis=axis_no))], axis=axis_no
    )


def shift_down(source, axis_no):
    lower_part = lax.slice_in_dim(source, 0, source.shape[axis_no] - 1, axis=axis_no)
    return jnp.concatenate(
        [jnp.zeros_like(lax.slice_in_dim(source, 0, 1, axis=axis_no)), lower_part], axis=axis_no
    )


def forward(charge):
    layers, rows, cols = charge.shape
    row_parts = lax.axis_size("bx")
    col_parts = lax.axis_size("by")
    row_me = lax.axis_index("bx")
    col_me = lax.axis_index("by")
    row_sub = rows // row_parts
    col_sub = cols // col_parts
    grid_x = rows * row_parts
    grid_y = cols * col_parts
    block = layers * rows
    lined = lax.all_to_all(
        charge.reshape(1, layers, row_parts, row_sub, cols),
        "bx",
        split_axis=2,
        concat_axis=0,
        tiled=True,
    )
    lined = lined.reshape(row_parts, layers * row_sub * cols)
    part_rows = jnp.arange(row_parts, dtype=jnp.int32)
    cos_table, sin_table = phase_table(part_rows[:, None], part_rows[None, :], row_parts, -1.0)
    real_part = jnp.einsum("ib,ik->kb", lined, cos_table, precision=highest)
    imag_part = jnp.einsum("ib,ik->kb", lined, sin_table, precision=highest)
    local_rows = row_me * row_sub + jnp.arange(row_sub, dtype=jnp.int32)
    cos_table, sin_table = phase_table(
        part_rows[:, None, None, None], local_rows[None, None, :, None], grid_x, -1.0
    )
    real_part, imag_part = rotate(
        real_part.reshape(row_parts, layers, row_sub, cols),
        imag_part.reshape(row_parts, layers, row_sub, cols),
        cos_table,
        sin_table,
    )
    stacked = jnp.stack([real_part, imag_part]).reshape(2, row_parts, layers, 1, row_sub, cols)
    stacked = lax.all_to_all(stacked, "bx", split_axis=1, concat_axis=3, tiled=True)
    stacked = stacked.reshape(2, layers, rows, cols)
    all_rows = jnp.arange(rows, dtype=jnp.int32)
    cos_table, sin_table = phase_table(all_rows[:, None], all_rows[None, :], rows, -1.0)
    real_part, imag_part = mix("lrs,rk->slk", stacked[0], stacked[1], cos_table, sin_table)
    stacked = jnp.stack([real_part, imag_part]).reshape(2, 1, col_parts, col_sub, block)
    stacked = lax.all_to_all(stacked, "by", split_axis=2, concat_axis=1, tiled=True)
    stacked = stacked.reshape(2, col_parts, col_sub, block)
    part_cols = jnp.arange(col_parts, dtype=jnp.int32)
    cos_table, sin_table = phase_table(part_cols[:, None], part_cols[None, :], col_parts, -1.0)
    real_part, imag_part = mix("jtb,jk->ktb", stacked[0], stacked[1], cos_table, sin_table)
    local_cols = col_me * col_sub + jnp.arange(col_sub, dtype=jnp.int32)
    cos_table, sin_table = phase_table(
        part_cols[:, None, None], local_cols[None, :, None], grid_y, -1.0
    )
    real_part, imag_part = rotate(real_part, imag_part, cos_table, sin_table)
    stacked = lax.all_to_all(
        jnp.stack([real_part, imag_part]), "by", split_axis=1, concat_axis=2, tiled=True
    )
    stacked = stacked.reshape(2, cols, block)
    all_cols = jnp.arange(cols, dtype=jnp.int32)
    cos_table, sin_table = phase_table(all_cols[:, None], all_cols[None, :], cols, -1.0)
    real_part, imag_part = mix("sb,sk->kb", stacked[0], stacked[1], cos_table, sin_table)
    return jnp.stack([real_part, imag_part]).reshape(2, cols, layers, rows)


def inverse(spectra):
    fields = spectra.shape[0]
    cols = spectra.shape[2]
    layers = spectra.shape[3]
    rows = spectra.shape[4]
    row_parts = lax.axis_size("bx")
    col_parts = lax.axis_size("by")
    row_me = lax.axis_index("bx")
    col_me = lax.axis_index("by")
    row_sub = rows // row_parts
    col_sub = cols // col_parts
    grid_x = rows * row_parts
    grid_y = cols * col_parts
    block = layers * rows
    all_cols = jnp.arange(cols, dtype=jnp.int32)
    cos_table, sin_table = phase_table(all_cols[:, None], all_cols[None, :], cols, 1.0)
    real_part, imag_part = mix(
        "fkb,ks->fsb",
        spectra[:, 0].reshape(fields, cols, block),
        spectra[:, 1].reshape(fields, cols, block),
        cos_table,
        sin_table,
    )
    cos_table, sin_table = phase_table(col_me, all_cols, grid_y, 1.0)
    real_part, imag_part = rotate(
        real_part, imag_part, cos_table[None, :, None], sin_table[None, :, None]
    )
    stacked = jnp.stack([real_part, imag_part], axis=1).reshape(
        fields, 2, 1, col_parts, col_sub, block
    )
    stacked = lax.all_to_all(stacked, "by", split_axis=3, concat_axis=2, tiled=True)
    stacked = stacked.reshape(fields, 2, col_parts, col_sub, block)
    part_cols = jnp.arange(col_parts, dtype=jnp.int32)
    cos_table, sin_table = phase_table(part_cols[:, None], part_cols[None, :], col_parts, 1.0)
    real_part, imag_part = mix("fktb,kj->fjtb", stacked[:, 0], stacked[:, 1], cos_table, sin_table)
    stacked = lax.all_to_all(
        jnp.stack([real_part, imag_part], axis=1), "by", split_axis=2, concat_axis=3, tiled=True
    )
    stacked = stacked.reshape(fields, 2, cols, layers, rows)
    all_rows = jnp.arange(rows, dtype=jnp.int32)
    cos_table, sin_table = phase_table(all_rows[:, None], all_rows[None, :], rows, 1.0)
    real_part, imag_part = mix("fslk,kr->flrs", stacked[:, 0], stacked[:, 1], cos_table, sin_table)
    cos_table, sin_table = phase_table(row_me, all_rows, grid_x, 1.0)
    real_part, imag_part = rotate(
        real_part, imag_part, cos_table[None, None, :, None], sin_table[None, None, :, None]
    )
    stacked = jnp.stack([real_part, imag_part], axis=1).reshape(
        fields, 2, 1, layers, row_parts, row_sub, cols
    )
    stacked = lax.all_to_all(stacked, "bx", split_axis=4, concat_axis=2, tiled=True)
    stacked = stacked.reshape(fields, 2, row_parts, layers * row_sub * cols)
    part_rows = jnp.arange(row_parts, dtype=jnp.int32)
    cos_table, sin_table = phase_table(part_rows[:, None], part_rows[None, :], row_parts, 1.0)
    real_out = jnp.einsum("fkb,ki->fib", stacked[:, 0], cos_table, precision=highest) - jnp.einsum(
        "fkb,ki->fib", stacked[:, 1], sin_table, precision=highest
    )
    real_out = real_out.reshape(fields, row_parts, layers, 1, row_sub, cols)
    real_out = lax.all_to_all(real_out, "bx", split_axis=1, concat_axis=3, tiled=True)
    return real_out.reshape(fields, layers, rows, cols) * (1.0 / (grid_x * grid_y))


def frequencies(rows, cols):
    row_parts = lax.axis_size("bx")
    col_parts = lax.axis_size("by")
    freq_x = (lax.axis_index("bx") + row_parts * jnp.arange(rows, dtype=jnp.int32)).astype(
        jnp.float32
    )
    freq_y = (lax.axis_index("by") + col_parts * jnp.arange(cols, dtype=jnp.int32)).astype(
        jnp.float32
    )
    return (freq_x[None, :], freq_y[:, None], rows * row_parts, cols * col_parts)


def solve(spectrum, freq_x, freq_y, grid_x, grid_y, permittivity, interfaces):
    layers = spectrum.shape[2]
    wave_x = jnp.sin(jnp.pi * freq_x / grid_x)
    wave_y = jnp.sin(jnp.pi * freq_y / grid_y)
    lateral = 4.0 * wave_x**2 + 4.0 * wave_y**2
    ratios = []
    primes = []
    for layer_no in range(layers):
        diagonal = (
            permittivity[layer_no] * lateral + interfaces[layer_no] + interfaces[layer_no + 1]
        )
        source = spectrum[:, :, layer_no, :]
        if layer_no == 0:
            pivot_now = diagonal
            primed = source / pivot_now
        else:
            pivot_now = diagonal - interfaces[layer_no] * ratios[-1]
            primed = (source + interfaces[layer_no] * primes[-1]) / pivot_now
        primes.append(primed)
        ratios.append(interfaces[layer_no + 1] / pivot_now)
    values = [primes[-1]]
    for layer_no in range(layers - 2, -1, -1):
        values.insert(0, primes[layer_no] + ratios[layer_no] * values[0])
    return jnp.stack(values, axis=2)


def back_transform(spectra):
    return inverse(spectra)


def evolve(padded, alpha_field, landau, stiffness, field_now):
    centre = padded[:, :, 1:-1, 1:-1]
    squares = centre * centre
    total = squares[0] + squares[1] + squares[2]
    quartic = landau[0][None, :, None, None]
    mixed = landau[1][None, :, None, None]
    sextic = landau[2][None, :, None, None]
    kappa = stiffness[None, :, None, None]
    lateral = (
        padded[:, :, 2:, 1:-1]
        + padded[:, :, :-2, 1:-1]
        + padded[:, :, 1:-1, 2:]
        + padded[:, :, 1:-1, :-2]
        - 4.0 * centre
    )
    vertical = shift_up(centre, 1) + shift_down(centre, 1) - 2.0 * centre
    drive = (
        2.0 * alpha_field[None] * centre
        + 4.0 * quartic * centre * squares
        + 2.0 * mixed * centre * (total[None] - squares)
        + 6.0 * sextic * centre * squares * squares
    )
    smooth = kappa * (lateral + vertical)
    return centre - step_size * (drive - smooth - field_now)


def shards(polarization, alpha_field, landau, stiffness, permittivity, interfaces):
    polar_now = polarization
    field_now = jnp.zeros_like(polarization)
    for step_no in range(STEPS):
        padded = extended(polar_now, (("bx", 2), ("by", 3)), 1)
        along_px = padded[0]
        along_py = padded[1]
        charge = -(
            0.5 * (along_px[:, 2:, 1:-1] - along_px[:, :-2, 1:-1])
            + 0.5 * (along_py[:, 1:-1, 2:] - along_py[:, 1:-1, :-2])
            + 0.5 * (shift_up(polar_now[2], 0) - shift_down(polar_now[2], 0))
        )
        spectrum = forward(charge)
        freq_x, freq_y, grid_x, grid_y = frequencies(charge.shape[1], charge.shape[2])
        potential_hat = solve(spectrum, freq_x, freq_y, grid_x, grid_y, permittivity, interfaces)
        potential = back_transform(potential_hat[None])[0]
        rimmed = extended(potential, (("bx", 1), ("by", 2)), 1)
        along_x = -0.5 * (rimmed[:, 2:, 1:-1] - rimmed[:, :-2, 1:-1])
        along_y = -0.5 * (rimmed[:, 1:-1, 2:] - rimmed[:, 1:-1, :-2])
        along_z = -0.5 * (shift_up(potential, 0) - shift_down(potential, 0))
        field_now = jnp.stack([along_x, along_y, along_z])
        polar_now = evolve(padded, alpha_field, landau, stiffness, field_now)
    return (polar_now, field_now)


def solution(mesh):
    return jax.shard_map(
        shards,
        mesh=mesh,
        in_specs=(P(None, None, "bx", "by"), P(None, "bx", "by"), P(), P(), P(), P()),
        out_specs=(P(None, None, "bx", "by"), P(None, None, "bx", "by")),
        check_vma=False,
    )
```

profile of v0, /device:TPU:0, one launch (start us, length us, event | category | flops | bytes accessed | tf_op | source)
XLA Modules:
  0.0 288.9 jit_solution(10470602075415794099)
XLA Ops:
  0.6 1.2 copy.169
  1.9 3.0 %collective-permute-start.1 = (f32[3,8,1,128]{3,1,2,0:T(8,128)S(1)}, f32[3,8,1,128]{3,1,2,0:T(8,128)S(1)}, u32[]{:S(2)}, u32[]{:S(2)}) collective-permute-start(f32[3,8,1,128]{3,1,2,0:T(8,128)S(1)} %get-tuple-element.49), channel_id=1, source_target_pairs={{0,4},{4,8},{8,12},{12,16},{16,20},{20,24},{24,28},{28,0},{1,5},{5... | collective-permute-start | bytes 36872 | tf_op jit(solution)/shard_map/ppermute | solution.py:19
  4.9 3.1 %collective-permute-start = (f32[3,8,1,128]{3,1,2,0:T(8,128)S(1)}, f32[3,8,1,128]{3,1,2,0:T(8,128)S(1)}, u32[]{:S(2)}, u32[]{:S(2)}) collective-permute-start(f32[3,8,1,128]{3,1,2,0:T(8,128)S(1)} %get-tuple-element.48), channel_id=1, source_target_pairs={{4,0},{8,4},{12,8},{16,12},{20,16},{24,20},{28,24},{0,28},{5,1},{9... | collective-permute-start | bytes 36872 | tf_op jit(solution)/shard_map/ppermute | solution.py:22
  8.1 1.6 collective-permute-done.1
  11.1 0.9 fusion.594
  12.5 9.0 %collective-permute-done.2 = f32[3,8,34,1]{3,1,2,0:T(8,128)S(1)} collective-permute-done((f32[3,8,34,1]{3,1,2,0:T(8,128)}, f32[3,8,34,1]{3,1,2,0:T(8,128)S(1)}, u32[]{:S(2)}, u32[]{:S(2)}) %collective-permute-start.2) | collective-permute-done | bytes 3296 | tf_op jit(solution)/shard_map/ppermute | solution.py:22
  21.6 2.1 collective-permute-done.3
  24.1 0.7 copy.140
  24.8 5.1 %all-to-all-start = ((f32[1,8,8,4,128]{4,3,1,0,2:T(4,128)}), f32[1,8,8,4,128]{4,3,1,0,2:T(4,128)S(1)}, u32[]{:S(2)}, u32[]{:S(2)}) async-start(f32[1,8,8,4,128]{4,3,1,0,2:T(4,128)} %copy.140), calls=%async_computation | async-start | bytes 262144 | tf_op jit(solution)/shard_map/all_to_all | solution.py:75
  30.1 7.2 %all-to-all-done = f32[1,8,8,4,128]{4,3,1,0,2:T(4,128)S(1)} async-done(((f32[1,8,8,4,128]{4,3,1,0,2:T(4,128)}), f32[1,8,8,4,128]{4,3,1,0,2:T(4,128)S(1)}, u32[]{:S(2)}, u32[]{:S(2)}) %all-to-all-start) | async-done | bytes 131104 | tf_op jit(solution)/shard_map/all_to_all | solution.py:75
  38.0 0.8 copy.141
  38.8 3.5 %all-to-all-start.1 = ((f32[2,8,8,1,4,128]{5,4,2,0,3,1:T(4,128)}), f32[2,8,8,1,4,128]{5,4,2,0,3,1:T(4,128)S(1)}, u32[]{:S(2)}, u32[]{:S(2)}) async-start(f32[2,8,8,1,4,128]{5,4,2,0,3,1:T(4,128)} %copy.141), calls=%async_computation.1 | async-start | bytes 524288 | tf_op jit(solution)/shard_map/all_to_all | solution.py:98
  43.7 0.7 fusion.614
  44.4 6.1 %all-to-all-done.1 = f32[2,8,8,1,4,128]{5,4,2,0,3,1:T(4,128)S(1)} async-done(((f32[2,8,8,1,4,128]{5,4,2,0,3,1:T(4,128)}), f32[2,8,8,1,4,128]{5,4,2,0,3,1:T(4,128)S(1)}, u32[]{:S(2)}, u32[]{:S(2)}) %all-to-all-start.1) | async-done | bytes 262176 | tf_op jit(solution)/shard_map/all_to_all | solution.py:98
  53.0 0.7 copy.149
  53.7 3.4 %all-to-all-start.2 = ((f32[2,1,4,32,256]{4,3,1,0,2:T(8,128)}), f32[2,1,4,32,256]{4,3,1,0,2:T(8,128)S(1)}, u32[]{:S(2)}, u32[]{:S(2)}) async-start(f32[2,1,4,32,256]{4,3,1,0,2:T(8,128)} %copy.149), calls=%async_computation.2 | async-start | bytes 524288 | tf_op jit(solution)/shard_map/all_to_all | solution.py:104
  57.3 5.8 %all-to-all-done.2 = f32[2,1,4,32,256]{4,3,1,0,2:T(8,128)S(1)} async-done(((f32[2,1,4,32,256]{4,3,1,0,2:T(8,128)}), f32[2,1,4,32,256]{4,3,1,0,2:T(8,128)S(1)}, u32[]{:S(2)}, u32[]{:S(2)}) %all-to-all-start.2) | async-done | bytes 262176 | tf_op jit(solution)/shard_map/all_to_all | solution.py:104
  65.0 0.8 copy.152
  65.7 3.4 %all-to-all-start.3 = ((f32[2,4,32,256]{3,2,0,1:T(8,128)}), f32[2,4,32,256]{3,2,0,1:T(8,128)S(1)}, u32[]{:S(2)}, u32[]{:S(2)}) async-start(f32[2,4,32,256]{3,2,0,1:T(8,128)} %copy.152), calls=%async_computation.3 | async-start | bytes 524288 | tf_op jit(solution)/shard_map/all_to_all | solution.py:114
  69.1 10.8 %fusion.201 = (f32[128,32]{0,1:T(8,128)S(1)}, f32[128,32]{0,1:T(8,128)S(1)}, f32[128,32]{0,1:T(8,128)S(1)}, f32[128,32]{0,1:T(8,128)S(1)}, f32[128,32]{0,1:T(8,1...) fusion(f32[]{:T(128)} %bitcast.54, f32[]{:T(128)} %bitcast.53, ...), kind=kLoop, calls=%fused_computation.396 | loop fusion | flops 188416 | bytes 246468 | tf_op jit(solution)/shard_map/sub | solution.py:213
  82.5 3.2 %fusion.143 = (f32[2,128,1,32]{1,3,2,0:T(8,128)S(1)}, f32[2,128,1,32]{1,3,2,0:T(8,128)S(1)}, f32[2,128,1,32]{1,3,2,0:T(8,128)S(1)}, f32[2,128,1,32]{1,3,2,0:T(8,128)S(1)}, f32[2,128,1,32]{1,3,2,0:T(8,128)S(1)}) fusion(f32[1,128,8,32]{1,3,2,0:T(8,128)S(1)} %bitcast.443, f32[1,128,8,32]{1,3,2,0:T(8,128)S(1)} %bitcast.445, ...), kind=kLoop, calls=%fused_computation.334 | loop fusion | flops 180224 | bytes 524308 | tf_op jit(solution)/shard_map/div | solution.py:214
  85.7 1.4 constant_dynamic-update-slice_fusion.10
  89.5 9.1 %all_to_all.180 = f32[1,2,1,4,32,256]{5,4,1,2,0,3:T(8,128)S(1)} all-to-all(f32[1,2,1,4,32,256]{5,4,1,2,0,3:T(8,128)S(1)} %pad_maximum_fusion.22), channel_id=1, replica_groups=mesh['bx'=8,'by'=4] {'by'}, dimensions={3} | all-to-all | bytes 524288 | tf_op jit(solution)/shard_map/all_to_all | solution.py:154
  100.5 0.8 copy.160
  101.2 3.5 %all-to-all-start.5 = ((f32[1,2,4,32,256]{4,3,1,0,2:T(8,128)}), f32[1,2,4,32,256]{4,3,1,0,2:T(8,128)S(1)}, u32[]{:S(2)}, u32[]{:S(2)}) async-start(f32[1,2,4,32,256]{4,3,1,0,2:T(8,128)} %copy.160), calls=%async_computation.5 | async-start | bytes 524288 | tf_op jit(solution)/shard_map/all_to_all | solution.py:159
  104.8 0.7 copy.122
  106.2 4.6 %all-to-all-done.5 = f32[1,2,4,32,256]{4,3,1,0,2:T(8,128)S(1)} async-done(((f32[1,2,4,32,256]{4,3,1,0,2:T(8,128)}), f32[1,2,4,32,256]{4,3,1,0,2:T(8,128)S(1)}, u32[]{:S(2)}, u32[]{:S(2)}) %all-to-all-start.5) | async-done | bytes 262176 | tf_op jit(solution)/shard_map/all_to_all | solution.py:159
  113.8 0.8 copy.205
  114.5 3.6 %all-to-all-start.6 = ((f32[1,2,1,8,8,4,128]{6,5,3,1,2,0,4:T(4,128)}), f32[1,2,1,8,8,4,128]{6,5,3,1,2,0,4:T(4,128)S(1)}, u32[]{:S(2)}, u32[]{:S(2)}) async-start(f32[1,2,1,8,8,4,128]{6,5,3,1,2,0,4:T(4,128)} %copy.205), calls=%async_computation.6 | async-start | bytes 524288 | tf_op jit(solution)/shard_map/all_to_all | solution.py:173
  118.8 8.1 %all-to-all-done.6 = f32[1,2,1,8,8,4,128]{6,5,3,1,2,0,4:T(4,128)S(1)} async-done(((f32[1,2,1,8,8,4,128]{6,5,3,1,2,0,4:T(4,128)}), f32[1,2,1,8,8,4,128]{6,5,3,1,2,0,4:T(4,128)S(1)}, u32[]{:S(2)}, u32[]{:S(2)}) %all-to-all-start.6) | async-done | bytes 262176 | tf_op jit(solution)/shard_map/all_to_all | solution.py:173
  128.3 3.5 %all-to-all-start.7 = ((f32[1,8,8,1,4,128]{5,4,2,3,0,1:T(4,128)}), f32[1,8,8,1,4,128]{5,4,2,3,0,1:T(4,128)S(1)}, u32[]{:S(2)}, u32[]{:S(2)}) async-start(f32[1,8,8,1,4,128]{5,4,2,3,0,1:T(4,128)} %copy.167), calls=%async_computation.7 | async-start | bytes 262144 | tf_op jit(solution)/shard_map/all_to_all | solution.py:181
  132.6 6.7 %all-to-all-done.7 = f32[1,8,8,1,4,128]{5,4,2,3,0,1:T(4,128)S(1)} async-done(((f32[1,8,8,1,4,128]{5,4,2,3,0,1:T(4,128)}), f32[1,8,8,1,4,128]{5,4,2,3,0,1:T(4,128)S(1)}, u32[]{:S(2)}, u32[]{:S(2)}) %all-to-all-start.7) | async-done | bytes 131104 | tf_op jit(solution)/shard_map/all_to_all | solution.py:181
  139.2 1.1 collective-permute-start.4
  140.4 0.9 collective-permute-start.5
  141.3 1.6 collective-permute-done.4
  142.9 3.8 %collective-permute-done.5 = f32[8,1,128]{2,0,1:T(8,128)S(1)} collective-permute-done((f32[8,1,128]{2,0,1:T(8,128)S(1)}, f32[8,1,128]{2,0,1:T(8,128)S(1)}, u32[]{:S(2)}, u32[]{:S(2)}) %collective-permute-start.5) | collective-permute-done | bytes 4128 | tf_op jit(solution)/shard_map/ppermute | solution.py:19
  147.4 3.3 %collective-permute-done.6 = f32[8,34,1]{2,0,1:T(8,128)S(1)} collective-permute-done((f32[8,34,1]{2,0,1:T(8,128)S(1)}, f32[8,34,1]{2,0,1:T(8,128)S(1)}, u32[]{:S(2)}, u32[]{:S(2)}) %collective-permute-start.6) | collective-permute-done | bytes 1120 | tf_op jit(solution)/shard_map/ppermute | solution.py:22
  150.7 1.5 collective-permute-done.7
  153.7 2.0 collective-permute-start.9
  155.7 1.7 collective-permute-done.8
  157.4 2.8 collective-permute-done.9
  160.9 8.8 %collective-permute-done.10 = f32[3,8,34,1]{3,1,2,0:T(8,128)S(1)} collective-permute-done((f32[3,8,34,1]{3,1,2,0:T(8,128)S(1)}, f32[3,8,34,1]{3,1,2,0:T(8,128)S(1)}, u32[]{:S(2)}, u32[]{:S(2)}) %collective-permute-start.10) | collective-permute-done | bytes 3296 | tf_op jit(solution)/shard_map/ppermute | solution.py:22
  169.7 2.5 collective-permute-done.11
  172.7 9.7 %all_to_all.181 = f32[1,8,8,4,128]{4,3,1,0,2:T(4,128)S(1)} all-to-all(f32[1,8,8,4,128]{4,3,1,0,2:T(4,128)S(1)} %copy.170), channel_id=1, replica_groups=mesh['bx'=8,'by'=4] {'bx'}, dimensions={2} | all-to-all | bytes 262144 | tf_op jit(solution)/shard_map/all_to_all | solution.py:75
  183.2 11.2 %all_to_all.182 = f32[2,8,8,1,4,128]{5,4,2,0,3,1:T(4,128)S(1)} all-to-all(f32[2,8,8,1,4,128]{5,4,2,0,3,1:T(4,128)S(1)} %copy.171), channel_id=1, replica_groups=mesh['bx'=8,'by'=4] {'bx'}, dimensions={1} | all-to-all | bytes 524288 | tf_op jit(solution)/shard_map/all_to_all | solution.py:98
  196.9 8.4 %all_to_all.183 = f32[2,1,4,32,256]{4,3,1,0,2:T(8,128)S(1)} all-to-all(f32[2,1,4,32,256]{4,3,1,0,2:T(8,128)S(1)} %copy.179), channel_id=1, replica_groups=mesh['bx'=8,'by'=4] {'by'}, dimensions={2} | all-to-all | bytes 524288 | tf_op jit(solution)/shard_map/all_to_all | solution.py:104
  207.5 8.4 %all_to_all.184 = f32[2,4,32,256]{3,2,0,1:T(8,128)S(1)} all-to-all(f32[2,4,32,256]{3,2,0,1:T(8,128)S(1)} %copy.182), channel_id=1, replica_groups=mesh['bx'=8,'by'=4] {'by'}, dimensions={1} | all-to-all | bytes 524288 | tf_op jit(solution)/shard_map/all_to_all | solution.py:114
  219.0 3.2 %fusion.123 = (f32[2,128,1,32]{1,3,2,0:T(8,128)S(1)}, f32[2,128,1,32]{1,3,2,0:T(8,128)S(1)}, f32[2,128,1,32]{1,3,2,0:T(8,128)S(1)}, f32[2,128,1,32]{1,3,2,0:T(8,128)S(1)}, f32[2,128,1,32]{1,3,2,0:T(8,128)S(1)}) fusion(f32[1,128,8,32]{1,3,2,0:T(8,128)S(1)} %bitcast.439, f32[1,128,8,32]{1,3,2,0:T(8,128)S(1)} %bitcast.441, f32[128,32]{0,1:T(8,128)S(1)} %copy-done.26, ...), kind=kLoop, calls=%fused_computation.314 | loop fusion | flops 180224 | bytes 524308 | tf_op jit(solution)/shard_map/div | solution.py:214
  222.3 1.4 constant_dynamic-update-slice_fusion.18
  226.1 8.4 %all_to_all.185 = f32[1,2,1,4,32,256]{5,4,1,2,0,3:T(8,128)S(1)} all-to-all(f32[1,2,1,4,32,256]{5,4,1,2,0,3:T(8,128)S(1)} %pad_maximum_fusion.27), channel_id=1, replica_groups=mesh['bx'=8,'by'=4] {'by'}, dimensions={3} | all-to-all | bytes 524288 | tf_op jit(solution)/shard_map/all_to_all | solution.py:154
  236.5 8.4 %all_to_all.186 = f32[1,2,4,32,256]{4,3,1,0,2:T(8,128)S(1)} all-to-all(f32[1,2,4,32,256]{4,3,1,0,2:T(8,128)S(1)} %copy.190), channel_id=1, replica_groups=mesh['bx'=8,'by'=4] {'by'}, dimensions={2} | all-to-all | bytes 524288 | tf_op jit(solution)/shard_map/all_to_all | solution.py:159
  247.5 0.8 copy.208
  248.3 3.6 %all-to-all-start.14 = ((f32[1,2,1,8,8,4,128]{6,5,3,1,2,0,4:T(4,128)}), f32[1,2,1,8,8,4,128]{6,5,3,1,2,0,4:T(4,128)S(1)}, u32[]{:S(2)}, u32[]{:S(2)}) async-start(f32[1,2,1,8,8,4,128]{6,5,3,1,2,0,4:T(4,128)} %copy.208), calls=%async_computation.14 | async-start | bytes 524288 | tf_op jit(solution)/shard_map/all_to_all | solution.py:173
  251.9 8.5 %all-to-all-done.14 = f32[1,2,1,8,8,4,128]{6,5,3,1,2,0,4:T(4,128)S(1)} async-done(((f32[1,2,1,8,8,4,128]{6,5,3,1,2,0,4:T(4,128)}), f32[1,2,1,8,8,4,128]{6,5,3,1,2,0,4:T(4,128)S(1)}, u32[]{:S(2)}, u32[]{:S(2)}) %all-to-all-start.14) | async-done | bytes 262176 | tf_op jit(solution)/shard_map/all_to_all | solution.py:173
  261.9 3.6 %all-to-all-start.15 = ((f32[1,8,8,1,4,128]{5,4,2,3,0,1:T(4,128)}), f32[1,8,8,1,4,128]{5,4,2,3,0,1:T(4,128)S(1)}, u32[]{:S(2)}, u32[]{:S(2)}) async-start(f32[1,8,8,1,4,128]{5,4,2,3,0,1:T(4,128)} %copy.197), calls=%async_computation.15 | async-start | bytes 262144 | tf_op jit(solution)/shard_map/all_to_all | solution.py:181
  266.1 6.7 %all-to-all-done.15 = f32[1,8,8,1,4,128]{5,4,2,3,0,1:T(4,128)S(1)} async-done(((f32[1,8,8,1,4,128]{5,4,2,3,0,1:T(4,128)}), f32[1,8,8,1,4,128]{5,4,2,3,0,1:T(4,128)S(1)}, u32[]{:S(2)}, u32[]{:S(2)}) %all-to-all-start.15) | async-done | bytes 131104 | tf_op jit(solution)/shard_map/all_to_all | solution.py:181
  272.8 1.1 collective-permute-start.12
  274.0 0.9 collective-permute-start.13
  274.9 1.6 collective-permute-done.12
  276.5 3.8 %collective-permute-done.13 = f32[8,1,128]{2,0,1:T(8,128)S(1)} collective-permute-done((f32[8,1,128]{2,0,1:T(8,128)S(1)}, f32[8,1,128]{2,0,1:T(8,128)S(1)}, u32[]{:S(2)}, u32[]{:S(2)}) %collective-permute-start.13) | collective-permute-done | bytes 4128 | tf_op jit(solution)/shard_map/ppermute | solution.py:19
  281.0 3.2 %collective-permute-done.14 = f32[8,34,1]{2,0,1:T(8,128)S(1)} collective-permute-done((f32[8,34,1]{2,0,1:T(8,128)S(1)}, f32[8,34,1]{2,0,1:T(8,128)S(1)}, u32[]{:S(2)}, u32[]{:S(2)}) %collective-permute-start.14) | collective-permute-done | bytes 1120 | tf_op jit(solution)/shard_map/ppermute | solution.py:22
  284.2 1.6 collective-permute-done.15
  286.1 0.8 copy.200
  288.1 0.8 copy.199
  (297 shorter events, 44.8 us)
Async XLA Ops:
  1.9 8.4 %copy-start = (f32[3,8,32,128]{3,2,1,0:T(8,128)S(1)}, f32[3,8,32,128]{3,2,1,0:T(8,128)}, u32[]{:S(2)}) copy-start(f32[3,8,32,128]{3,2,1,0:T(8,128)} %param.6) | copy-start | bytes 1179652
  1.9 7.8 %collective-permute-start.1 = (f32[3,8,1,128]{3,1,2,0:T(8,128)S(1)}, f32[3,8,1,128]{3,1,2,0:T(8,128)S(1)}, u32[]{:S(2)}, u32[]{:S(2)}) collective-permute-start(f32[3,8,1,128]{3,1,2,0:T(8,128)S(1)} %get-tuple-element.49), channel_id=1, source_target_pairs={{0,4},{4,8},{8,12},{12,16},{16,20},{20,24},{24,28},{28,0},{1,5},{5... | collective-permute-start | bytes 36872 | tf_op jit(solution)/shard_map/ppermute | solution.py:19
  4.9 5.6 %collective-permute-start = (f32[3,8,1,128]{3,1,2,0:T(8,128)S(1)}, f32[3,8,1,128]{3,1,2,0:T(8,128)S(1)}, u32[]{:S(2)}, u32[]{:S(2)}) collective-permute-start(f32[3,8,1,128]{3,1,2,0:T(8,128)S(1)} %get-tuple-element.48), channel_id=1, source_target_pairs={{4,0},{8,4},{12,8},{16,12},{20,16},{24,20},{28,24},{0,28},{5,1},{9... | collective-permute-start | bytes 36872 | tf_op jit(solution)/shard_map/ppermute | solution.py:22
  12.0 9.6 %collective-permute-start.2 = (f32[3,8,34,1]{3,1,2,0:T(8,128)}, f32[3,8,34,1]{3,1,2,0:T(8,128)S(1)}, u32[]{:S(2)}, u32[]{:S(2)}) collective-permute-start(f32[3,8,34,1]{3,1,2,0:T(8,128)} %get-tuple-element.35), channel_id=1, source_target_pairs={{1,0},{2,1},{3,2},{0,3},{5,4},{6,5},{7,6},{4,7},{9,8},{10,9},{11,1... | collective-permute-start | bytes 9800 | tf_op jit(solution)/shard_map/ppermute | solution.py:22
  12.0 11.6 %collective-permute-start.3 = (f32[3,8,34,1]{3,1,2,0:T(8,128)S(1)}, f32[3,8,34,1]{3,1,2,0:T(8,128)S(1)}, u32[]{:S(2)}, u32[]{:S(2)}) collective-permute-start(f32[3,8,34,1]{3,1,2,0:T(8,128)S(1)} %get-tuple-element.34), channel_id=1, source_target_pairs={{0,1},{1,2},{2,3},{3,0},{4,5},{5,6},{6,7},{7,4},{8,9},{9,10},{10,1... | collective-permute-start | bytes 9800 | tf_op jit(solution)/shard_map/ppermute | solution.py:19
  24.8 12.5 %all-to-all-start = ((f32[1,8,8,4,128]{4,3,1,0,2:T(4,128)}), f32[1,8,8,4,128]{4,3,1,0,2:T(4,128)S(1)}, u32[]{:S(2)}, u32[]{:S(2)}) async-start(f32[1,8,8,4,128]{4,3,1,0,2:T(4,128)} %copy.140), calls=%async_computation | async-start | bytes 262144 | tf_op jit(solution)/shard_map/all_to_all | solution.py:75
  38.8 5.0 %copy-start.40 = (f32[9]{0:T(128)S(1)}, f32[9]{0:T(128)}, u32[]{:S(2)}) copy-start(f32[9]{0:T(128)} %param.11) | copy-start | bytes 112
  38.8 11.8 %all-to-all-start.1 = ((f32[2,8,8,1,4,128]{5,4,2,0,3,1:T(4,128)}), f32[2,8,8,1,4,128]{5,4,2,0,3,1:T(4,128)S(1)}, u32[]{:S(2)}, u32[]{:S(2)}) async-start(f32[2,8,8,1,4,128]{5,4,2,0,3,1:T(4,128)} %copy.141), calls=%async_computation.1 | async-start | bytes 524288 | tf_op jit(solution)/shard_map/all_to_all | solution.py:98
  42.4 46.5 %copy-start.48 = (f32[128]{0:T(128)}, f32[128]{0:T(128)S(1)}, u32[]{:S(2)}) copy-start(f32[128]{0:T(128)S(1)} %fusion.338) | copy-start | bytes 1540
  43.1 45.8 %copy-start.50 = (f32[128]{0:T(128)}, f32[128]{0:T(128)S(1)}, u32[]{:S(2)}) copy-start(f32[128]{0:T(128)S(1)} %get-tuple-element.142) | copy-start | bytes 1540
  53.7 9.4 %all-to-all-start.2 = ((f32[2,1,4,32,256]{4,3,1,0,2:T(8,128)}), f32[2,1,4,32,256]{4,3,1,0,2:T(8,128)S(1)}, u32[]{:S(2)}, u32[]{:S(2)}) async-start(f32[2,1,4,32,256]{4,3,1,0,2:T(8,128)} %copy.149), calls=%async_computation.2 | async-start | bytes 524288 | tf_op jit(solution)/shard_map/all_to_all | solution.py:104
  57.3 7.1 %copy-start.27 = (f32[4,32]{0,1:T(8,128)}, f32[4,32]{0,1:T(8,128)S(1)}, u32[]{:S(2)}) copy-start(f32[4,32]{0,1:T(8,128)S(1)} %get-tuple-element.137) | copy-start | bytes 1540
  57.3 7.1 %copy-start.29 = (f32[4,32]{0,1:T(8,128)}, f32[4,32]{0,1:T(8,128)S(1)}, u32[]{:S(2)}) copy-start(f32[4,32]{0,1:T(8,128)S(1)} %get-tuple-element.138) | copy-start | bytes 1540
  65.7 14.3 %all-to-all-start.3 = ((f32[2,4,32,256]{3,2,0,1:T(8,128)}), f32[2,4,32,256]{3,2,0,1:T(8,128)S(1)}, u32[]{:S(2)}, u32[]{:S(2)}) async-start(f32[2,4,32,256]{3,2,0,1:T(8,128)} %copy.152), calls=%async_computation.3 | async-start | bytes 524288 | tf_op jit(solution)/shard_map/all_to_all | solution.py:114
  79.9 2.5 copy-start.17
  79.9 2.5 copy-start.19
  79.9 2.5 copy-start.21
  79.9 2.5 copy-start.23
  80.0 2.5 copy-start.25
  80.0 5.7 %copy-start.5 = (f32[128,32]{0,1:T(8,128)}, f32[128,32]{0,1:T(8,128)S(1)}, u32[]{:S(2)}) copy-start(f32[128,32]{0,1:T(8,128)S(1)} %get-tuple-element.105) | copy-start | bytes 49156
  80.0 5.7 %copy-start.7 = (f32[128,32]{0,1:T(8,128)}, f32[128,32]{0,1:T(8,128)S(1)}, u32[]{:S(2)}) copy-start(f32[128,32]{0,1:T(8,128)S(1)} %get-tuple-element.107) | copy-start | bytes 49156
  80.0 5.7 %copy-start.9 = (f32[128,32]{0,1:T(8,128)}, f32[128,32]{0,1:T(8,128)S(1)}, u32[]{:S(2)}) copy-start(f32[128,32]{0,1:T(8,128)S(1)} %get-tuple-element.109) | copy-start | bytes 49156
  80.0 5.7 %copy-start.11 = (f32[128,32]{0,1:T(8,128)}, f32[128,32]{0,1:T(8,128)S(1)}, u32[]{:S(2)}) copy-start(f32[128,32]{0,1:T(8,128)S(1)} %get-tuple-element.110) | copy-start | bytes 49156
  80.0 5.7 %copy-start.13 = (f32[128,32]{0,1:T(8,128)}, f32[128,32]{0,1:T(8,128)S(1)}, u32[]{:S(2)}) copy-start(f32[128,32]{0,1:T(8,128)S(1)} %get-tuple-element.116) | copy-start | bytes 49156
  80.0 5.7 %copy-start.15 = (f32[128,32]{0,1:T(8,128)}, f32[128,32]{0,1:T(8,128)S(1)}, u32[]{:S(2)}) copy-start(f32[128,32]{0,1:T(8,128)S(1)} %get-tuple-element.119) | copy-start | bytes 49156
  101.2 3.6 %copy-start.31 = (f32[8,32,128]{2,1,0:T(8,128)S(1)}, f32[8,32,128]{2,1,0:T(8,128)}, u32[]{:S(2)}) copy-start(f32[8,32,128]{2,1,0:T(8,128)} %param.7) | copy-start | bytes 393220
  101.2 9.5 %all-to-all-start.5 = ((f32[1,2,4,32,256]{4,3,1,0,2:T(8,128)}), f32[1,2,4,32,256]{4,3,1,0,2:T(8,128)S(1)}, u32[]{:S(2)}, u32[]{:S(2)}) async-start(f32[1,2,4,32,256]{4,3,1,0,2:T(8,128)} %copy.160), calls=%async_computation.5 | async-start | bytes 524288 | tf_op jit(solution)/shard_map/all_to_all | solution.py:159
  114.5 3.6 %copy-start.58 = (f32[3,8]{1,0:T(4,128)S(1)}, f32[3,8]{1,0:T(4,128)}, u32[]{:S(2)}) copy-start(f32[3,8]{1,0:T(4,128)} %param.8) | copy-start | bytes 292
  114.5 12.4 %all-to-all-start.6 = ((f32[1,2,1,8,8,4,128]{6,5,3,1,2,0,4:T(4,128)}), f32[1,2,1,8,8,4,128]{6,5,3,1,2,0,4:T(4,128)S(1)}, u32[]{:S(2)}, u32[]{:S(2)}) async-start(f32[1,2,1,8,8,4,128]{6,5,3,1,2,0,4:T(4,128)} %copy.205), calls=%async_computation.6 | async-start | bytes 524288 | tf_op jit(solution)/shard_map/all_to_all | solution.py:173
  128.3 10.9 %all-to-all-start.7 = ((f32[1,8,8,1,4,128]{5,4,2,3,0,1:T(4,128)}), f32[1,8,8,1,4,128]{5,4,2,3,0,1:T(4,128)S(1)}, u32[]{:S(2)}, u32[]{:S(2)}) async-start(f32[1,8,8,1,4,128]{5,4,2,3,0,1:T(4,128)} %copy.167), calls=%async_computation.7 | async-start | bytes 262144 | tf_op jit(solution)/shard_map/all_to_all | solution.py:181
  139.2 3.7 %collective-permute-start.4 = (f32[8,1,128]{2,0,1:T(8,128)S(1)}, f32[8,1,128]{2,0,1:T(8,128)S(1)}, u32[]{:S(2)}, u32[]{:S(2)}) collective-permute-start(f32[8,1,128]{2,0,1:T(8,128)S(1)} %get-tuple-element.99), channel_id=1, source_target_pairs={{4,0},{8,4},{12,8},{16,12},{20,16},{24,20},{28,24},{0,28},{5,1},{9... | collective-permute-start | bytes 12296 | tf_op jit(solution)/shard_map/ppermute | solution.py:22
  140.4 6.3 %collective-permute-start.5 = (f32[8,1,128]{2,0,1:T(8,128)S(1)}, f32[8,1,128]{2,0,1:T(8,128)S(1)}, u32[]{:S(2)}, u32[]{:S(2)}) collective-permute-start(f32[8,1,128]{2,0,1:T(8,128)S(1)} %get-tuple-element.98), channel_id=1, source_target_pairs={{0,4},{4,8},{8,12},{12,16},{16,20},{20,24},{24,28},{28,0},{1,5},{5... | collective-permute-start | bytes 12296 | tf_op jit(solution)/shard_map/ppermute | solution.py:19
  146.8 3.9 %collective-permute-start.6 = (f32[8,34,1]{2,0,1:T(8,128)S(1)}, f32[8,34,1]{2,0,1:T(8,128)S(1)}, u32[]{:S(2)}, u32[]{:S(2)}) collective-permute-start(f32[8,34,1]{2,0,1:T(8,128)S(1)} %get-tuple-element.92), channel_id=1, source_target_pairs={{1,0},{2,1},{3,2},{0,3},{5,4},{6,5},{7,6},{4,7},{9,8},{10,9},{11,1... | collective-permute-start | bytes 3272 | tf_op jit(solution)/shard_map/ppermute | solution.py:22
  146.9 5.3 %collective-permute-start.7 = (f32[8,34,1]{2,0,1:T(8,128)S(1)}, f32[8,34,1]{2,0,1:T(8,128)S(1)}, u32[]{:S(2)}, u32[]{:S(2)}) collective-permute-start(f32[8,34,1]{2,0,1:T(8,128)S(1)} %get-tuple-element.93), channel_id=1, source_target_pairs={{0,1},{1,2},{2,3},{3,0},{4,5},{5,6},{6,7},{7,4},{8,9},{9,10},{10,1... | collective-permute-start | bytes 3272 | tf_op jit(solution)/shard_map/ppermute | solution.py:19
  147.4 5.0 %copy-start.1 = (f32[8,32,128]{2,0,1:T(8,128)S(1)}, f32[8,32,128]{2,0,1:T(8,128)}, u32[]{:S(2)}) copy-start(f32[8,32,128]{2,0,1:T(8,128)} %copy.122) | copy-start | bytes 393220
  147.4 5.0 %copy-start.3 = (f32[8,32,128]{2,0,1:T(8,128)S(1)}, f32[8,32,128]{2,0,1:T(8,128)}, u32[]{:S(2)}) copy-start(f32[8,32,128]{2,0,1:T(8,128)} %fusion.57) | copy-start | bytes 393220
  153.6 3.7 %collective-permute-start.8 = (f32[3,8,1,128]{3,1,2,0:T(8,128)S(1)}, f32[3,8,1,128]{3,1,2,0:T(8,128)S(1)}, u32[]{:S(2)}, u32[]{:S(2)}) collective-permute-start(f32[3,8,1,128]{3,1,2,0:T(8,128)S(1)} %get-tuple-element.41), channel_id=1, source_target_pairs={{4,0},{8,4},{12,8},{16,12},{20,16},{24,20},{28,24},{0,28},{5,1},{9... | collective-permute-start | bytes 36872 | tf_op jit(solution)/shard_map/ppermute | solution.py:22
  153.7 6.4 %collective-permute-start.9 = (f32[3,8,1,128]{3,1,2,0:T(8,128)S(1)}, f32[3,8,1,128]{3,1,2,0:T(8,128)S(1)}, u32[]{:S(2)}, u32[]{:S(2)}) collective-permute-start(f32[3,8,1,128]{3,1,2,0:T(8,128)S(1)} %get-tuple-element.40), channel_id=1, source_target_pairs={{0,4},{4,8},{8,12},{12,16},{16,20},{20,24},{24,28},{28,0},{1,5},{5... | collective-permute-start | bytes 36872 | tf_op jit(solution)/shard_map/ppermute | solution.py:19
  157.4 14.8 %copy-start.32 = (f32[3,8,1,128]{3,1,2,0:T(8,128)}, f32[3,8,1,128]{3,1,2,0:T(8,128)S(1)}, u32[]{:S(2)}) copy-start(f32[3,8,1,128]{3,1,2,0:T(8,128)S(1)} %collective-permute-done.8) | copy-start | bytes 36868
  160.1 12.0 %copy-start.34 = (f32[3,8,1,128]{3,1,2,0:T(8,128)}, f32[3,8,1,128]{3,1,2,0:T(8,128)S(1)}, u32[]{:S(2)}) copy-start(f32[3,8,1,128]{3,1,2,0:T(8,128)S(1)} %collective-permute-done.9) | copy-start | bytes 36868
  160.3 9.3 %collective-permute-start.10 = (f32[3,8,34,1]{3,1,2,0:T(8,128)S(1)}, f32[3,8,34,1]{3,1,2,0:T(8,128)S(1)}, u32[]{:S(2)}, u32[]{:S(2)}) collective-permute-start(f32[3,8,34,1]{3,1,2,0:T(8,128)S(1)} %get-tuple-element.32), channel_id=1, source_target_pairs={{1,0},{2,1},{3,2},{0,3},{5,4},{6,5},{7,6},{4,7},{9,8},{10,9},{11,1... | collective-permute-start | bytes 9800 | tf_op jit(solution)/shard_map/ppermute | solution.py:22
  160.4 11.7 %collective-permute-start.11 = (f32[3,8,34,1]{3,1,2,0:T(8,128)S(1)}, f32[3,8,34,1]{3,1,2,0:T(8,128)S(1)}, u32[]{:S(2)}, u32[]{:S(2)}) collective-permute-start(f32[3,8,34,1]{3,1,2,0:T(8,128)S(1)} %get-tuple-element.33), channel_id=1, source_target_pairs={{0,1},{1,2},{2,3},{3,0},{4,5},{5,6},{6,7},{7,4},{8,9},{9,10},{10,1... | collective-permute-start | bytes 9800 | tf_op jit(solution)/shard_map/ppermute | solution.py:19
  206.2 0.7 copy-start.30
  218.2 0.7 copy-start.20
  218.2 0.7 copy-start.22
  218.2 0.7 copy-start.24
  218.2 0.7 copy-start.26
  219.0 3.3 %copy-start.6 = (f32[128,32]{0,1:T(8,128)S(1)}, f32[128,32]{0,1:T(8,128)}, u32[]{:S(2)}) copy-start(f32[128,32]{0,1:T(8,128)} %copy-done.5) | copy-start | bytes 49156
  219.0 3.3 %copy-start.8 = (f32[128,32]{0,1:T(8,128)S(1)}, f32[128,32]{0,1:T(8,128)}, u32[]{:S(2)}) copy-start(f32[128,32]{0,1:T(8,128)} %copy-done.7) | copy-start | bytes 49156
  219.0 3.3 %copy-start.10 = (f32[128,32]{0,1:T(8,128)S(1)}, f32[128,32]{0,1:T(8,128)}, u32[]{:S(2)}) copy-start(f32[128,32]{0,1:T(8,128)} %copy-done.9) | copy-start | bytes 49156
  219.0 3.3 %copy-start.12 = (f32[128,32]{0,1:T(8,128)S(1)}, f32[128,32]{0,1:T(8,128)}, u32[]{:S(2)}) copy-start(f32[128,32]{0,1:T(8,128)} %copy-done.11) | copy-start | bytes 49156
  219.0 3.3 %copy-start.14 = (f32[128,32]{0,1:T(8,128)S(1)}, f32[128,32]{0,1:T(8,128)}, u32[]{:S(2)}) copy-start(f32[128,32]{0,1:T(8,128)} %copy-done.13) | copy-start | bytes 49156
  219.0 3.3 %copy-start.16 = (f32[128,32]{0,1:T(8,128)S(1)}, f32[128,32]{0,1:T(8,128)}, u32[]{:S(2)}) copy-start(f32[128,32]{0,1:T(8,128)} %copy-done.15) | copy-start | bytes 49156
  248.3 12.2 %all-to-all-start.14 = ((f32[1,2,1,8,8,4,128]{6,5,3,1,2,0,4:T(4,128)}), f32[1,2,1,8,8,4,128]{6,5,3,1,2,0,4:T(4,128)S(1)}, u32[]{:S(2)}, u32[]{:S(2)}) async-start(f32[1,2,1,8,8,4,128]{6,5,3,1,2,0,4:T(4,128)} %copy.208), calls=%async_computation.14 | async-start | bytes 524288 | tf_op jit(solution)/shard_map/all_to_all | solution.py:173
  261.9 10.9 %all-to-all-start.15 = ((f32[1,8,8,1,4,128]{5,4,2,3,0,1:T(4,128)}), f32[1,8,8,1,4,128]{5,4,2,3,0,1:T(4,128)S(1)}, u32[]{:S(2)}, u32[]{:S(2)}) async-start(f32[1,8,8,1,4,128]{5,4,2,3,0,1:T(4,128)} %copy.197), calls=%async_computation.15 | async-start | bytes 262144 | tf_op jit(solution)/shard_map/all_to_all | solution.py:181
  272.8 3.7 %collective-permute-start.12 = (f32[8,1,128]{2,0,1:T(8,128)S(1)}, f32[8,1,128]{2,0,1:T(8,128)S(1)}, u32[]{:S(2)}, u32[]{:S(2)}) collective-permute-start(f32[8,1,128]{2,0,1:T(8,128)S(1)} %get-tuple-element.95), channel_id=1, source_target_pairs={{4,0},{8,4},{12,8},{16,12},{20,16},{24,20},{28,24},{0,28},{5,1},{9... | collective-permute-start | bytes 12296 | tf_op jit(solution)/shard_map/ppermute | solution.py:22
  274.0 6.3 %collective-permute-start.13 = (f32[8,1,128]{2,0,1:T(8,128)S(1)}, f32[8,1,128]{2,0,1:T(8,128)S(1)}, u32[]{:S(2)}, u32[]{:S(2)}) collective-permute-start(f32[8,1,128]{2,0,1:T(8,128)S(1)} %get-tuple-element.94), channel_id=1, source_target_pairs={{0,4},{4,8},{8,12},{12,16},{16,20},{20,24},{24,28},{28,0},{1,5},{5... | collective-permute-start | bytes 12296 | tf_op jit(solution)/shard_map/ppermute | solution.py:19
  280.4 3.8 %collective-permute-start.14 = (f32[8,34,1]{2,0,1:T(8,128)S(1)}, f32[8,34,1]{2,0,1:T(8,128)S(1)}, u32[]{:S(2)}, u32[]{:S(2)}) collective-permute-start(f32[8,34,1]{2,0,1:T(8,128)S(1)} %get-tuple-element.88), channel_id=1, source_target_pairs={{1,0},{2,1},{3,2},{0,3},{5,4},{6,5},{7,6},{4,7},{9,8},{10,9},{11,1... | collective-permute-start | bytes 3272 | tf_op jit(solution)/shard_map/ppermute | solution.py:22
  280.4 5.4 %collective-permute-start.15 = (f32[8,34,1]{2,0,1:T(8,128)S(1)}, f32[8,34,1]{2,0,1:T(8,128)S(1)}, u32[]{:S(2)}, u32[]{:S(2)}) collective-permute-start(f32[8,34,1]{2,0,1:T(8,128)S(1)} %get-tuple-element.89), channel_id=1, source_target_pairs={{0,1},{1,2},{2,3},{3,0},{4,5},{5,6},{6,7},{7,4},{8,9},{9,10},{10,1... | collective-permute-start | bytes 3272 | tf_op jit(solution)/shard_map/ppermute | solution.py:19
  286.0 0.9 copy-start.57
  286.0 0.9 copy-start.2
  286.0 1.0 copy-start.4
  286.1 1.0 copy-start.33
  286.1 0.9 copy-start.35
  (20 other events, 13.4 us)
where the time goes:
time: 291 us; the launch traced here: 289 us
  waiting for transfers between devices  102 us (35%)
  blocking collectives  63.6 us (22%)
  starting transfers between devices  47.9 us (16%)
  other arithmetic  26.2 us (9%)
  matrix products  23.5 us (8%)
  local copies, waits for them, and re-layouts  23.1 us (8%)
    ppermute x8, waiting for transfers between devices, extended(): lax.ppermute(lax.slice_in_dim(block, 0, width, axis=dim), axis, backward)  29 us
    ppermute x8, waiting for transfers between devices, extended(): lax.ppermute(lax.slice_in_dim(block, block.shape[dim] - width, None, axis...  19.5 us
    all_to_all x2, blocking collectives, inverse(): lax.all_to_all(stacked, 'by', split_axis=3, concat_axis=2, tiled=True)  17.5 us
    all_to_all x2, waiting for transfers between devices, inverse(): lax.all_to_all(stacked, 'bx', split_axis=4, concat_axis=2, tiled=True)  16.7 us
    all_to_all x2, waiting for transfers between devices, inverse(): lax.all_to_all(real_out, 'bx', split_axis=1, concat_axis=3, tiled=True)  13.3 us
    all_to_all x1, blocking collectives, forward(): lax.all_to_all(stacked, 'bx', split_axis=1, concat_axis=3, tiled=True)  11.2 us
    sub x1, other arithmetic, solve(): pivot_now = diagonal - interfaces[layer_no] * ratios[-1]  10.8 us
    all_to_all x1, blocking collectives, forward(): lax.all_to_all(charge.reshape(1, layers, row_parts, row_sub, cols), 'bx',...  9.74 us
  transfers between devices with their start and end apart: 25, of which 23 were waited for; matrix products, arithmetic and copies ran while one was open for 6% of the time, Pallas kernels for 0%

commit v1 on v0

v1 whole, which is shorter than its diff:
```python
import functools

import jax
import jax.numpy as jnp
from jax import lax
from jax.experimental import pallas as pl
from jax.experimental.pallas import tpu as pltpu
from jax.sharding import PartitionSpec as P

STEPS = 2
step_size = 0.05
MESH = pl.DeviceIdType.MESH
PAD = 8


def cas_table(left, right, length):
    turns = left * right % length
    angle = 2.0 * jnp.pi / length * turns.astype(jnp.float32)
    table = jnp.cos(angle) + jnp.sin(angle)
    high = lax.reduce_precision(table, 8, 7)
    return jnp.stack([high.astype(jnp.bfloat16), (table - high).astype(jnp.bfloat16)])


def halves(value):
    high = value.astype(jnp.bfloat16)
    low = (value - high.astype(jnp.float32)).astype(jnp.bfloat16)
    return high, low


def product(left, right):
    dot = functools.partial(jnp.dot, preferred_element_type=jnp.float32)
    return dot(left[0], right[0]) + (dot(left[0], right[1]) + dot(left[1], right[0]))


def kernel(sizes, p_in, alpha, landau, stiff, perm, inter, lam, hx, hy, p_out, f_out, *scratch):
    L, R, C, nbx, nby, rep, lp, own = sizes
    (p_mid, base, coef, ratio, q, inb, outs, rec_f, rec_i, ybuf, phat, u,
     row_s, row_r, col_s, col_r, pc_s, pc_r, ssem, rsem) = scratch
    R2 = R + PAD
    bx = lax.axis_index("bx")
    by = lax.axis_index("by")
    group = bx // rep
    part = bx % rep
    scale = 1.0 / (R * nbx * C * nby)
    slots = [0]
    sends = []

    barrier = pltpu.get_barrier_semaphore()
    for k in range(1, nbx):
        pl.semaphore_signal(barrier, inc=1, device_id={"bx": (bx + k) % nbx}, device_id_type=MESH)
    for k in range(1, nby):
        pl.semaphore_signal(barrier, inc=1, device_id={"by": (by + k) % nby}, device_id_type=MESH)

    def remote(src, dst, device, slot):
        return pltpu.make_async_remote_copy(
            src_ref=src, dst_ref=dst, send_sem=ssem.at[slot], recv_sem=rsem.at[slot],
            device_id=device, device_id_type=MESH)

    def fresh():
        slots[0] += 1
        return slots[0] - 1

    def push(src, dst, device):
        copy = remote(src, dst, device, fresh())
        copy.start()
        sends.append(copy.wait_send)
        return copy

    rows = lax.broadcasted_iota(jnp.int32, (R, C), 0)
    lanes = lax.broadcasted_iota(jnp.int32, (R, C), 1)

    def x_next(f, high):
        return jnp.where(rows == R - 1, high, pltpu.roll(f, R - 1, 0))

    def x_prev(f, low):
        return jnp.where(rows == 0, low, pltpu.roll(f, 1, 0))

    def y_next(f, high):
        return jnp.where(lanes == C - 1, high, pltpu.roll(f, C - 1, 1))

    def y_prev(f, low):
        return jnp.where(lanes == 0, low, pltpu.roll(f, 1, 1))

    def column_tile(blocks):
        tile = jnp.zeros((R, C), jnp.float32)
        for at, block in enumerate(blocks):
            tile = jnp.where(lanes == at, block[:, 0:1], tile)
            tile = jnp.where(lanes == C // 2 + at, block[:, C - 1:C], tile)
        return tile

    def x_start(src, n):
        mine = inb.at[n, :, pl.ds(pl.multiple_of(bx * R, R), R)]
        copies = []
        for k in range(1, nbx):
            to = (bx + k) % nbx
            copies.append(push(src.at[pl.ds(to // rep * lp, lp)], mine, {"bx": to}))
        for layer in range(lp):
            inb[n, layer, pl.ds(pl.multiple_of(bx * R, R), R)] = src[group * lp + layer]
        return copies

    def x_finish(copies, n, dst, height):
        for copy in copies:
            copy.wait_recv()
        table = (hx[0], hx[1])
        for layer in range(lp):
            outs[n, :, layer] = product(table, halves(inb[n, layer])).reshape(own, R2, C)
        waits = []
        landing = dst.at[pl.ds(group * lp, lp)]
        for t in range(own):
            local = (group + t) % own
            to = part * own + local
            src = outs.at[n, local, :, pl.ds(0, height)]
            if rep == 1:
                if t == 0:
                    continue
                waits.append(push(src, landing, {"bx": to}).wait_recv)
                continue
            slot = fresh()

            def go(src=src, to=to, slot=slot):
                remote(src, landing, {"bx": to}, slot).start()

            def gone(src=src, to=to, slot=slot):
                @pl.when(to != bx)
                def _():
                    remote(src, landing, {"bx": to}, slot).wait_send()

            def came(src=src, to=to, slot=slot, t=t):
                origin = (bx % own + own - t) % own * rep + bx // own

                @pl.when(origin != bx)
                def _():
                    remote(src, landing, {"bx": to}, slot).wait_recv()

            pl.when(to != bx)(go)
            sends.append(gone)
            waits.append(came)

        def keep():
            for layer in range(lp):
                dst[group * lp + layer] = outs[n, bx % own, layer, 0:height]

        if rep == 1:
            keep()
        else:
            pl.when(bx // own == part)(keep)
        for wait in waits:
            wait()

    def y_pass(src, n):
        copies = [push(src, ybuf.at[n, k - 1], {"by": (by + k) % nby}) for k in range(1, nby)]
        total = product(halves(src[...].reshape(L * R, C)), (hy[0, by], hy[1, by]))
        for k in range(1, nby):
            copies[k - 1].wait_recv()
            origin = (by + nby - k) % nby
            total += product(halves(ybuf[n, k - 1].reshape(L * R, C)), (hy[0, origin], hy[1, origin]))
        return total

    def flank_start(rows_too, step, src):
        copies = []
        if rows_too:
            for c in range(3):
                for l in range(L):
                    at = c * L + l
                    row_s[step, 0, at:at + 1] = src[c, l, 0:1]
                    row_s[step, 1, at:at + 1] = src[c, l, R - 1:R]
            col_s[step] = column_tile([src[c, l] for c in range(3) for l in range(L)])
            if step == 0:
                pl.semaphore_wait(barrier, nbx + nby - 2)
            copies.append(push(row_s.at[step, 1], row_r.at[step, 0], {"bx": (bx + 1) % nbx}))
            copies.append(push(row_s.at[step, 0], row_r.at[step, 1], {"bx": (bx + nbx - 1) % nbx}))
            tile, land = col_s.at[step], col_r
        else:
            pc_s[step] = column_tile([src[l, 0:R] for l in range(L)])
            tile, land = pc_s.at[step], pc_r
        copies.append(push(tile, land.at[step, 0], {"by": (by + 1) % nby}))
        copies.append(push(tile, land.at[step, 1], {"by": (by + nby - 1) % nby}))
        return copies

    for step in range(STEPS):
        src = p_in if step == 0 else p_mid
        flanks = flank_start(True, step, src)
        if step == 0:
            lateral = lam[...]
            previous = None
            for l in range(L):
                pivot = perm[l] * lateral + inter[l] + inter[l + 1]
                if l:
                    pivot = pivot - inter[l] * previous
                inverse = 1.0 / pivot
                coef[l] = inverse
                previous = inter[l + 1] * inverse
                ratio[l] = previous
        for copy in flanks:
            copy.wait_recv()
        low_col = col_r[step, 0]
        high_col = col_r[step, 1]

        def edges(c, l):
            at = c * L + l
            return (row_r[step, 0, at:at + 1], row_r[step, 1, at:at + 1],
                    low_col[:, C // 2 + at:C // 2 + at + 1], high_col[:, at:at + 1])

        zero = jnp.zeros((R, C), jnp.float32)
        for l in range(L):
            low, high, _, _ = edges(0, l)
            _, _, left, right = edges(1, l)
            along_x, along_y = src[0, l], src[1, l]
            above = src[2, l + 1] if l + 1 < L else zero
            below = src[2, l - 1] if l else zero
            q[step, l] = -0.5 * (
                (x_next(along_x, high) - x_prev(along_x, low))
                + (y_next(along_y, right) - y_prev(along_y, left)) + (above - below))
        copies = x_start(q.at[step], 2 * step)
        for l in range(L):
            cells = [src[c, l] for c in range(3)]
            squares = [cell * cell for cell in cells]
            whole = squares[0] + squares[1] + squares[2]
            for c in range(3):
                cell, square = cells[c], squares[c]
                low, high, left, right = edges(c, l)
                above = src[c, l + 1] if l + 1 < L else zero
                below = src[c, l - 1] if l else zero
                smooth = stiff[l] * (
                    (x_next(cell, high) + x_prev(cell, low) + y_next(cell, right)
                     + y_prev(cell, left) - 4.0 * cell) + (above + below - 2.0 * cell))
                drive = cell * (
                    2.0 * alpha[l] + 4.0 * landau[0, l] * square
                    + 2.0 * landau[1, l] * (whole - square)
                    + 6.0 * landau[2, l] * (square * square))
                base[c, l] = cell - step_size * (drive - smooth)
        x_finish(copies, 2 * step, rec_f.at[step], R)
        spectrum = y_pass(rec_f.at[step], 2 * step)
        primes = []
        for l in range(L):
            source = spectrum[l * R:(l + 1) * R] * scale
            if l:
                source = source + inter[l] * primes[-1]
            primes.append(source * coef[l])
        value = primes[-1]
        phat[step, L - 1] = value
        for l in range(L - 2, -1, -1):
            value = primes[l] + ratio[l] * value
            phat[step, l] = value
        u[step] = y_pass(phat.at[step], 2 * step + 1).reshape(L, R, C)
        x_finish(x_start(u.at[step], 2 * step + 1), 2 * step + 1, rec_i.at[step], R2)
        flanks = flank_start(False, step, rec_i.at[step])
        last = step == STEPS - 1
        target = p_out if last else p_mid
        for l in range(L):
            phi = rec_i[step, l, 0:R]
            low = rec_i[step, l, R:R + 1]
            high = rec_i[step, l, R + 1:R + 2]
            along_x = -0.5 * (x_next(phi, high) - x_prev(phi, low))
            above = rec_i[step, l + 1, 0:R] if l + 1 < L else zero
            below = rec_i[step, l - 1, 0:R] if l else zero
            along_z = -0.5 * (above - below)
            target[0, l] = base[0, l] + step_size * along_x
            target[2, l] = base[2, l] + step_size * along_z
            if last:
                f_out[0, l] = along_x
                f_out[2, l] = along_z
        for copy in flanks:
            copy.wait_recv()
        low_phi = pc_r[step, 0]
        high_phi = pc_r[step, 1]
        for l in range(L):
            phi = rec_i[step, l, 0:R]
            along_y = -0.5 * (y_next(phi, high_phi[:, l:l + 1])
                              - y_prev(phi, low_phi[:, C // 2 + l:C // 2 + l + 1]))
            target[1, l] = base[1, l] + step_size * along_y
            if last:
                f_out[1, l] = along_y
    for wait in sends:
        wait()


def shards(polarization, alpha_field, landau, stiffness, permittivity, interfaces):
    _, L, R, C = polarization.shape
    nbx = lax.axis_size("bx")
    nby = lax.axis_size("by")
    bx = lax.axis_index("bx")
    by = lax.axis_index("by")
    rep = max(1, nbx // L)
    lp = max(1, L // nbx)
    own = nbx // rep
    grid_x, grid_y = nbx * R, nby * C
    R2 = R + PAD
    line = jnp.arange(R2, dtype=jnp.int32)
    line = jnp.where(line < R, line, jnp.where(line == R, -1, R))
    owners = bx % rep * own + jnp.arange(own, dtype=jnp.int32)
    wanted = ((owners[:, None] * R + line[None, :] + grid_x) % grid_x).reshape(own * R2, 1)
    hx = cas_table(wanted, jnp.arange(grid_x, dtype=jnp.int32)[None, :], grid_x)
    my_cols = by * C + jnp.arange(C, dtype=jnp.int32)
    hy = cas_table(jnp.arange(grid_y, dtype=jnp.int32)[:, None], my_cols[None, :], grid_y)
    hy = hy.reshape(2, nby, C, C)
    my_rows = bx * R + jnp.arange(R, dtype=jnp.int32)
    wave_x = jnp.sin(jnp.pi * my_rows.astype(jnp.float32) / grid_x)
    wave_y = jnp.sin(jnp.pi * my_cols.astype(jnp.float32) / grid_y)
    lam = 4.0 * wave_x[:, None] ** 2 + 4.0 * wave_y[None, :] ** 2
    sizes = (L, R, C, nbx, nby, rep, lp, own)
    n_copies = STEPS * (6 + 2 * (nbx - 1 + own + nby - 1))
    f32 = jnp.float32
    vmem = pl.BlockSpec(memory_space=pltpu.VMEM)
    smem = pl.BlockSpec(memory_space=pltpu.SMEM)
    S = STEPS
    scratch = [
        pltpu.VMEM((3, L, R, C), f32), pltpu.VMEM((3, L, R, C), f32),
        pltpu.VMEM((L, R, C), f32), pltpu.VMEM((L, R, C), f32),
        pltpu.VMEM((S, L, R, C), f32), pltpu.VMEM((2 * S, lp, grid_x, C), f32),
        pltpu.VMEM((2 * S, own, lp, R2, C), f32), pltpu.VMEM((S, L, R, C), f32),
        pltpu.VMEM((S, L, R2, C), f32), pltpu.VMEM((2 * S, nby - 1, L, R, C), f32),
        pltpu.VMEM((S, L, R, C), f32), pltpu.VMEM((S, L, R, C), f32),
        pltpu.VMEM((S, 2, 3 * L, C), f32), pltpu.VMEM((S, 2, 3 * L, C), f32),
        pltpu.VMEM((S, R, C), f32), pltpu.VMEM((S, 2, R, C), f32),
        pltpu.VMEM((S, R, C), f32), pltpu.VMEM((S, 2, R, C), f32),
        pltpu.SemaphoreType.DMA((n_copies,)), pltpu.SemaphoreType.DMA((n_copies,)),
    ]
    out = jax.ShapeDtypeStruct(polarization.shape, f32)
    return pl.pallas_call(
        functools.partial(kernel, sizes),
        out_shape=(out, out),
        in_specs=[vmem, vmem, smem, smem, smem, smem, vmem, vmem, vmem],
        out_specs=(vmem, vmem),
        scratch_shapes=scratch,
        compiler_params=pltpu.CompilerParams(
            collective_id=0, has_side_effects=True, vmem_limit_bytes=48 * 1024 * 1024),
    )(polarization, alpha_field, landau, stiffness, permittivity, interfaces, lam, hx, hy)


def solution(mesh):
    return jax.shard_map(
        shards,
        mesh=mesh,
        in_specs=(P(None, None, "bx", "by"), P(None, "bx", "by"), P(), P(), P(), P()),
        out_specs=(P(None, None, "bx", "by"), P(None, None, "bx", "by")),
        check_vma=False,
    )
```

time: 291 us -> 90.5 us (0.31)
  waiting for transfers between devices: 102 us -> 0 us
  Pallas kernels: 0 us -> 83.9 us
  blocking collectives: 63.6 us -> 0 us
  starting transfers between devices: 47.9 us -> 0 us
  matrix products: 23.5 us -> 0 us
  other arithmetic: 26.2 us -> 3.15 us
  local copies, waits for them, and re-layouts: 23.1 us -> 2.52 us
    pallas_call x0 -> x1, Pallas kernels: none -> 83.9 us  [shards(): pl.pallas_call(functools.partial(kernel, sizes), out_shape=(out, out), in...]
    all_to_all x7 -> x0, blocking collectives: 63.6 us -> none  [the longest x2 17.5 us: inverse(): lax.all_to_all(stacked, 'by', split_axis=3, concat_axis=2, tiled=True)]
    all_to_all x9 -> x0, waiting for transfers between devices: 53.7 us -> none  [the longest x2 16.7 us: inverse(): lax.all_to_all(stacked, 'bx', split_axis=4, concat_axis=2, tiled=True)]
    ppermute x16 -> x0, waiting for transfers between devices: 48.6 us -> none  [the longest x8 29 us: extended(): lax.ppermute(lax.slice_in_dim(block, 0, width, axis=dim), axis, backward)]
    all_to_all x9 -> x0, starting transfers between devices: 33.3 us -> none  [the longest x2 7.16 us: inverse(): lax.all_to_all(stacked, 'bx', split_axis=4, concat_axis=2, tiled=True)]
    dot_general x56 -> x0, matrix products: 23.5 us -> none  [the longest x12 5.31 us: mix(): jnp.einsum(form, imag_part, sin_table, precision=highest)]
    ppermute x16 -> x0, starting transfers between devices: 14.6 us -> none  [the longest x8 8.88 us: extended(): lax.ppermute(lax.slice_in_dim(block, block.shape[dim] - width, None, axis...]
    sub x4 -> x0, other arithmetic: 12.6 us -> none  [the longest x1 10.8 us: solve(): pivot_now = diagonal - interfaces[layer_no] * ratios[-1]]
  transfers between devices with their start and end apart: 25 -> 0, of which waited for: 23 -> 0; matrix products, arithmetic and copies ran while one was open for 6% -> 0% of each run, Pallas kernels for 0% -> 0%
where the time goes in v1:
time: 90.5 us; the launch traced here: 90.4 us
  Pallas kernels  83.9 us (93%)
  other arithmetic  3.15 us (3%)
  local copies, waits for them, and re-layouts  2.52 us (3%)
    pallas_call x1, Pallas kernels, shards(): pl.pallas_call(functools.partial(kernel, sizes), out_shape=(out, out), in...  83.9 us
    convert_element_type x2, other arithmetic, cas_table(): high.astype(jnp.bfloat16)  2.82 us
    unnamed x14, local copies, waits for them, and re-layouts  2.44 us

profile of v1, /device:TPU:0, one launch (start us, length us, event | category | flops | bytes accessed | tf_op | source)
XLA Modules:
  0.0 90.4 jit_solution(683303859268583220)
XLA Ops:
  0.8 0.1 add_add_fusion
  0.9 0.1 add.183
  0.9 0.1 broadcast_add_fusion.lam
  1.0 1.3 %reduce-precision_convert_fusion.1 = (bf16[1,4,128,128]{3,2,1,0:T(8,128)(2,1)S(1)}, bf16[1,4,128,128]{3,2,1,0:T(8,128)(2,1)S(1)}) fusion(s32[128]{0:T(128)S(1)} %iota_add_fusion, s32[4,128]{1,0:T(4,128)S(1)} %multiply_add_fusion), kind=kLoop, calls=%fused_computation.11 | loop fusion | flops 1245184 | bytes 264704 | tf_op jit(solution)/shard_map/convert_element_type | solution.py:21
  2.3 1.6 %reduce-precision_convert_fusion = (bf16[1,320,256]{2,1,0:T(8,128)(2,1)S(1)}, bf16[1,320,256]{2,1,0:T(8,128)(2,1)S(1)}) fusion(s32[320]{0:T(512)S(1)} %add_select_fusion.2), kind=kLoop, calls=%fused_computation.7 | loop fusion | flops 1556480 | bytes 328960 | tf_op jit(solution)/shard_map/convert_element_type | solution.py:21
  3.9 0.0 copy-start
  3.9 0.0 copy-start.1
  3.9 0.0 copy-start.2
  3.9 0.0 copy-start.3
  3.9 0.0 copy-start.4
  3.9 0.0 copy-start.5
  4.0 0.9 copy-done
  4.9 0.0 copy-done.1
  4.9 0.0 copy-done.2
  4.9 0.0 copy-done.3
  4.9 0.0 copy-done.4
  4.9 0.0 copy-done.5
  4.9 83.9 %shard_map.77 = (f32[3,8,32,128]{3,2,1,0:T(8,128)S(1)}, f32[3,8,32,128]{3,2,1,0:T(8,128)S(1)}) custom-call(f32[3,8,32,128]{3,2,1,0:T(8,128)S(1)} %copy-done, f32[8,32,128]{2,1,0:T(8,128)S(1)} %copy-done.1, f32[3,8]{1,0:T(4,128)S(1)} %copy-done.2, f32[8]{0:T(128)S(1)} %copy-done.3, f32[8]{0:T(128)S(1)} %copy-done.4, f32[9]{0:T(128)S(1)} %copy-done.5, ...), custom_call_target="tpu_custom_call" | custom-call | tf_op jit(solution)/shard_map/pallas_call | solution.py:320
  88.9 0.7 copy.10
  89.6 0.7 copy.11
  (9 shorter events, 0.2 us)
Async XLA Ops:
  3.9 1.0 %copy-start = (f32[3,8,32,128]{3,2,1,0:T(8,128)S(1)}, f32[3,8,32,128]{3,2,1,0:T(8,128)}, u32[]{:S(2)}) copy-start(f32[3,8,32,128]{3,2,1,0:T(8,128)} %p_in.1) | copy-start | bytes 1179652
  3.9 1.0 %copy-start.1 = (f32[8,32,128]{2,1,0:T(8,128)S(1)}, f32[8,32,128]{2,1,0:T(8,128)}, u32[]{:S(2)}) copy-start(f32[8,32,128]{2,1,0:T(8,128)} %alpha.1) | copy-start | bytes 393220
  3.9 1.0 %copy-start.2 = (f32[3,8]{1,0:T(4,128)S(1)}, f32[3,8]{1,0:T(4,128)}, u32[]{:S(2)}) copy-start(f32[3,8]{1,0:T(4,128)} %landau.1) | copy-start | bytes 292
  3.9 1.0 %copy-start.3 = (f32[8]{0:T(128)S(1)}, f32[8]{0:T(128)}, u32[]{:S(2)}) copy-start(f32[8]{0:T(128)} %stiff.1) | copy-start | bytes 100
  3.9 1.0 %copy-start.4 = (f32[8]{0:T(128)S(1)}, f32[8]{0:T(128)}, u32[]{:S(2)}) copy-start(f32[8]{0:T(128)} %perm.1) | copy-start | bytes 100
  3.9 1.0 %copy-start.5 = (f32[9]{0:T(128)S(1)}, f32[9]{0:T(128)}, u32[]{:S(2)}) copy-start(f32[9]{0:T(128)} %inter.1) | copy-start | bytes 112

commit v2 on v1

--- a/solution.py
+++ b/solution.py
@@ -2,6 +2,7 @@
 
 import jax
 import jax.numpy as jnp
+import numpy as np
 from jax import lax
 from jax.experimental import pallas as pl
 from jax.experimental.pallas import tpu as pltpu
@@ -21,6 +22,18 @@
     return jnp.stack([high.astype(jnp.bfloat16), (table - high).astype(jnp.bfloat16)])
 
 
+def fixed_table(left, right, length):
+    angle = 2.0 * np.pi / length * (left * right % length)
+    table = (np.cos(angle) + np.sin(angle)).astype(np.float32)
+    high = table.astype(jnp.bfloat16)
+    low = (table - high.astype(np.float32)).astype(jnp.bfloat16)
+    return jnp.asarray(np.stack([high, low]))
+
+
+def is_wide(rows, nbx, nby, layers):
+    return layers % nbx == 0 and rows % (8 * nby) == 0
+
+
 def halves(value):
     high = value.astype(jnp.bfloat16)
     low = (value - high.astype(jnp.float32)).astype(jnp.bfloat16)
@@ -34,8 +47,14 @@
 
 def kernel(sizes, p_in, alpha, landau, stiff, perm, inter, lam, hx, hy, p_out, f_out, *scratch):
     L, R, C, nbx, nby, rep, lp, own = sizes
-    (p_mid, base, coef, ratio, q, inb, outs, rec_f, rec_i, ybuf, phat, u,
-     row_s, row_r, col_s, col_r, pc_s, pc_r, ssem, rsem) = scratch
+    (p_mid, base, coef, ratio, q, inb, outs, rec_i,
+     row_s, row_r, col_s, col_r, pc_s, pc_r, ssem, rsem) = scratch[:16]
+    wide = is_wide(R, nbx, nby, L)
+    if wide:
+        z_in, w_out = scratch[16:]
+    else:
+        rec_f, ybuf, phat, u = scratch[16:]
+    thin = R // nby
     R2 = R + PAD
     bx = lax.axis_index("bx")
     by = lax.axis_index("by")
@@ -46,10 +65,12 @@
     sends = []
 
     barrier = pltpu.get_barrier_semaphore()
-    for k in range(1, nbx):
-        pl.semaphore_signal(barrier, inc=1, device_id={"bx": (bx + k) % nbx}, device_id_type=MESH)
-    for k in range(1, nby):
-        pl.semaphore_signal(barrier, inc=1, device_id={"by": (by + k) % nby}, device_id_type=MESH)
+    others = [(a, b) for b in range(nby) for a in range(nbx) if a or b]
+    greeted = [(a, b) for a, b in others if wide or not a or not b]
+    for a, b in greeted:
+        pl.semaphore_signal(
+            barrier, inc=1, device_id={"bx": (bx + a) % nbx, "by": (by + b) % nby},
+            device_id_type=MESH)
 
     def remote(src, dst, device, slot):
         return pltpu.make_async_remote_copy(
@@ -98,12 +119,51 @@
             inb[n, layer, pl.ds(pl.multiple_of(bx * R, R), R)] = src[group * lp + layer]
         return copies
 
-    def x_finish(copies, n, dst, height):
+    def x_mix(copies, n):
         for copy in copies:
             copy.wait_recv()
         table = (hx[0], hx[1])
         for layer in range(lp):
             outs[n, :, layer] = product(table, halves(inb[n, layer])).reshape(own, R2, C)
+
+    def spread(n, step):
+        copies = []
+        for a, b in others:
+            to_x, to_y = (bx + a) % nbx, (by + b) % nby
+            copies.append(push(
+                outs.at[n, to_x, :, pl.ds(pl.multiple_of(to_y * thin, thin), thin)],
+                z_in.at[step, by, pl.ds(bx * lp, lp)], {"bx": to_x, "by": to_y}))
+        for layer in range(lp):
+            z_in[step, by, bx * lp + layer] = outs[
+                n, bx, layer, pl.ds(pl.multiple_of(by * thin, thin), thin)]
+        for copy in copies:
+            copy.wait_recv()
+
+    def collect(n, step):
+        at = pl.ds(pl.multiple_of(bx * R + by * thin, thin), thin)
+        copies = []
+        for a, b in others:
+            to_x, to_y = (bx + a) % nbx, (by + b) % nby
+            copies.append(push(
+                w_out.at[step, to_y, pl.ds(to_x * lp, lp)], inb.at[n, :, at],
+                {"bx": to_x, "by": to_y}))
+        for layer in range(lp):
+            inb[n, layer, at] = w_out[step, by, bx * lp + layer]
+        return copies
+
+    def solve(spectrum, height):
+        primes = []
+        for l in range(L):
+            source = spectrum[l * height:(l + 1) * height] * scale
+            if l:
+                source = source + inter[l] * primes[-1]
+            primes.append(source * coef[l])
+        values = [primes[-1]]
+        for l in range(L - 2, -1, -1):
+            values.insert(0, primes[l] + ratio[l] * values[0])
+        return values
+
+    def x_finish(n, dst, height):
         waits = []
         landing = dst.at[pl.ds(group * lp, lp)]
         for t in range(own):
@@ -166,7 +226,7 @@
                     row_s[step, 1, at:at + 1] = src[c, l, R - 1:R]
             col_s[step] = column_tile([src[c, l] for c in range(3) for l in range(L)])
             if step == 0:
-                pl.semaphore_wait(barrier, nbx + nby - 2)
+                pl.semaphore_wait(barrier, len(greeted))
             copies.append(push(row_s.at[step, 1], row_r.at[step, 0], {"bx": (bx + 1) % nbx}))
             copies.append(push(row_s.at[step, 0], row_r.at[step, 1], {"bx": (bx + nbx - 1) % nbx}))
             tile, land = col_s.at[step], col_r
@@ -229,21 +289,26 @@
                     + 2.0 * landau[1, l] * (whole - square)
                     + 6.0 * landau[2, l] * (square * square))
                 base[c, l] = cell - step_size * (drive - smooth)
-        x_finish(copies, 2 * step, rec_f.at[step], R)
-        spectrum = y_pass(rec_f.at[step], 2 * step)
-        primes = []
-        for l in range(L):
-            source = spectrum[l * R:(l + 1) * R] * scale
-            if l:
-                source = source + inter[l] * primes[-1]
-            primes.append(source * coef[l])
-        value = primes[-1]
-        phat[step, L - 1] = value
-        for l in range(L - 2, -1, -1):
-            value = primes[l] + ratio[l] * value
-            phat[step, l] = value
-        u[step] = y_pass(phat.at[step], 2 * step + 1).reshape(L, R, C)
-        x_finish(x_start(u.at[step], 2 * step + 1), 2 * step + 1, rec_i.at[step], R2)
+        n = 2 * step
+        x_mix(copies, n)
+        if wide:
+            spread(n, step)
+            table = (hy[0], hy[1])
+            full = jnp.concatenate(
+                [z_in[step, j].reshape(L * thin, C) for j in range(nby)], axis=1)
+            values = solve(product(halves(full), table), thin)
+            full = product(halves(jnp.concatenate(values, axis=0)), table)
+            for j in range(nby):
+                w_out[step, j] = full[:, j * C:(j + 1) * C].reshape(L, thin, C)
+            copies = collect(n + 1, step)
+        else:
+            x_finish(n, rec_f.at[step], R)
+            for l, value in enumerate(solve(y_pass(rec_f.at[step], n), R)):
+                phat[step, l] = value
+            u[step] = y_pass(phat.at[step], n + 1).reshape(L, R, C)
+            copies = x_start(u.at[step], n + 1)
+        x_mix(copies, n + 1)
+        x_finish(n + 1, rec_i.at[step], R2)
         flanks = flank_start(False, step, rec_i.at[step])
         last = step == STEPS - 1
         target = p_out if last else p_mid
@@ -286,36 +351,52 @@
     own = nbx // rep
     grid_x, grid_y = nbx * R, nby * C
     R2 = R + PAD
-    line = jnp.arange(R2, dtype=jnp.int32)
-    line = jnp.where(line < R, line, jnp.where(line == R, -1, R))
-    owners = bx % rep * own + jnp.arange(own, dtype=jnp.int32)
+    wide = is_wide(R, nbx, nby, L)
+    pool = np if wide else jnp
+    make = fixed_table if wide else cas_table
+    line = pool.arange(R2, dtype=jnp.int32)
+    line = pool.where(line < R, line, pool.where(line == R, -1, R))
+    owners = pool.arange(own, dtype=jnp.int32)
+    if not wide:
+        owners = owners + bx % rep * own
     wanted = ((owners[:, None] * R + line[None, :] + grid_x) % grid_x).reshape(own * R2, 1)
-    hx = cas_table(wanted, jnp.arange(grid_x, dtype=jnp.int32)[None, :], grid_x)
+    hx = make(wanted, pool.arange(grid_x, dtype=jnp.int32)[None, :], grid_x)
+    every_col = pool.arange(grid_y, dtype=jnp.int32)
+    my_rows = bx * R + jnp.arange(R, dtype=jnp.int32)
     my_cols = by * C + jnp.arange(C, dtype=jnp.int32)
-    hy = cas_table(jnp.arange(grid_y, dtype=jnp.int32)[:, None], my_cols[None, :], grid_y)
-    hy = hy.reshape(2, nby, C, C)
-    my_rows = bx * R + jnp.arange(R, dtype=jnp.int32)
+    if wide:
+        hy = make(every_col[:, None], every_col[None, :], grid_y)
+        my_rows = bx * R + by * (R // nby) + jnp.arange(R // nby, dtype=jnp.int32)
+        my_cols = jnp.arange(grid_y, dtype=jnp.int32)
+    else:
+        hy = make(every_col[:, None], my_cols[None, :], grid_y).reshape(2, nby, C, C)
     wave_x = jnp.sin(jnp.pi * my_rows.astype(jnp.float32) / grid_x)
     wave_y = jnp.sin(jnp.pi * my_cols.astype(jnp.float32) / grid_y)
     lam = 4.0 * wave_x[:, None] ** 2 + 4.0 * wave_y[None, :] ** 2
     sizes = (L, R, C, nbx, nby, rep, lp, own)
-    n_copies = STEPS * (6 + 2 * (nbx - 1 + own + nby - 1))
+    n_copies = STEPS * (6 + 2 * (nbx * nby + own if wide else nbx + own + nby))
     f32 = jnp.float32
     vmem = pl.BlockSpec(memory_space=pltpu.VMEM)
     smem = pl.BlockSpec(memory_space=pltpu.SMEM)
     S = STEPS
     scratch = [
         pltpu.VMEM((3, L, R, C), f32), pltpu.VMEM((3, L, R, C), f32),
-        pltpu.VMEM((L, R, C), f32), pltpu.VMEM((L, R, C), f32),
+        pltpu.VMEM((L,) + lam.shape, f32), pltpu.VMEM((L,) + lam.shape, f32),
         pltpu.VMEM((S, L, R, C), f32), pltpu.VMEM((2 * S, lp, grid_x, C), f32),
-        pltpu.VMEM((2 * S, own, lp, R2, C), f32), pltpu.VMEM((S, L, R, C), f32),
-        pltpu.VMEM((S, L, R2, C), f32), pltpu.VMEM((2 * S, nby - 1, L, R, C), f32),
-        pltpu.VMEM((S, L, R, C), f32), pltpu.VMEM((S, L, R, C), f32),
+        pltpu.VMEM((2 * S, own, lp, R2, C), f32), pltpu.VMEM((S, L, R2, C), f32),
         pltpu.VMEM((S, 2, 3 * L, C), f32), pltpu.VMEM((S, 2, 3 * L, C), f32),
         pltpu.VMEM((S, R, C), f32), pltpu.VMEM((S, 2, R, C), f32),
         pltpu.VMEM((S, R, C), f32), pltpu.VMEM((S, 2, R, C), f32),
         pltpu.SemaphoreType.DMA((n_copies,)), pltpu.SemaphoreType.DMA((n_copies,)),
     ]
+    if wide:
+        thin = (S, nby, L, R // nby, C)
+        scratch += [pltpu.VMEM(thin, f32), pltpu.VMEM(thin, f32)]
+    else:
+        scratch += [
+            pltpu.VMEM((S, L, R, C), f32), pltpu.VMEM((2 * S, nby - 1, L, R, C), f32),
+            pltpu.VMEM((S, L, R, C), f32), pltpu.VMEM((S, L, R, C), f32),
+        ]
     out = jax.ShapeDtypeStruct(polarization.shape, f32)
     return pl.pallas_call(
         functools.partial(kernel, sizes),

time: 90.5 us -> 77 us (0.85); the launches traced: 90.4 us -> 75.8 us
  Pallas kernels: 83.9 us -> 68.7 us
  local copies, waits for them, and re-layouts: 2.52 us -> 6.19 us
  other arithmetic: 3.15 us -> 0.16 us
    pallas_call x1, Pallas kernels: 83.9 us -> 68.7 us  [shards(): pl.pallas_call(functools.partial(kernel, sizes), out_shape=(out, out), in...]
    unnamed x14 -> x18, local copies, waits for them, and re-layouts: 2.44 us -> 6.19 us
    convert_element_type x2 -> x0, other arithmetic: 2.82 us -> none  [cas_table(): high.astype(jnp.bfloat16)]
where the time goes in v2:
time: 77 us; the launch traced here: 75.8 us
  Pallas kernels  68.7 us (89%)
  local copies, waits for them, and re-layouts  6.19 us (8%)
    pallas_call x1, Pallas kernels, shards(): pl.pallas_call(functools.partial(kernel, sizes), out_shape=(out, out), in...  68.7 us
    unnamed x18, local copies, waits for them, and re-layouts  6.19 us

profile of v2, /device:TPU:0, one launch (start us, length us, event | category | flops | bytes accessed | tf_op | source)
XLA Modules:
  0.0 75.8 jit_solution(11793104047021479230)
XLA Ops:
  0.7 0.0 copy-start.4
  0.7 0.0 copy-start.5
  0.8 0.0 copy-start.6
  0.8 0.0 copy-start.7
  0.8 0.1 broadcast_add_fusion.lam
  0.9 0.6 copy-done.4
  1.4 0.0 copy-done.5
  1.4 0.0 copy-done.6
  1.4 0.0 copy-done.7
  1.4 0.0 copy-start
  1.4 1.2 %copy-done = bf16[2,512,512]{2,1,0:T(8,128)(2,1)S(1)} copy-done((bf16[2,512,512]{2,1,0:T(8,128)(2,1)S(1)}, bf16[2,512,512]{2,1,0:T(8,128)(2,1)}, u32[]{:S(2)}) %copy-start) | copy-done | bytes 1048600
  2.7 0.0 copy-start.1
  2.7 1.0 %copy-done.1 = f32[3,8,32,128]{3,2,1,0:T(8,128)S(1)} copy-done((f32[3,8,32,128]{3,2,1,0:T(8,128)S(1)}, f32[3,8,32,128]{3,2,1,0:T(8,128)}, u32[]{:S(2)}) %copy-start.1) | copy-done | bytes 393240
  3.7 0.0 copy-start.2
  3.7 1.0 %copy-done.2 = bf16[2,320,256]{2,1,0:T(8,128)(2,1)S(1)} copy-done((bf16[2,320,256]{2,1,0:T(8,128)(2,1)S(1)}, bf16[2,320,256]{2,1,0:T(8,128)(2,1)}, u32[]{:S(2)}) %copy-start.2) | copy-done | bytes 327704
  4.6 0.0 copy-start.3
  4.6 0.9 %copy-done.3 = f32[8,32,128]{2,1,0:T(8,128)S(1)} copy-done((f32[8,32,128]{2,1,0:T(8,128)S(1)}, f32[8,32,128]{2,1,0:T(8,128)}, u32[]{:S(2)}) %copy-start.3) | copy-done | bytes 131096
  5.5 68.7 %shard_map.95 = (f32[3,8,32,128]{3,2,1,0:T(8,128)S(1)}, f32[3,8,32,128]{3,2,1,0:T(8,128)S(1)}) custom-call(f32[3,8,32,128]{3,2,1,0:T(8,128)S(1)} %copy-done.1, f32[8,32,128]{2,1,0:T(8,128)S(1)} %copy-done.3, f32[3,8]{1,0:T(4,128)S(1)} %copy-done.4, f32[8]{0:T(128)S(1)} %copy-done.5, f32[8]{0:T(128)S(1)} %copy-done.6, f32[9]{0:T(128)S(1)} %copy-done.7, ...), custom_call_target="tpu_custom_call" | custom-call | tf_op jit(solution)/shard_map/pallas_call | solution.py:401
  74.3 0.7 copy.12
  75.0 0.7 copy.13
  (2 shorter events, 0.1 us)
Async XLA Ops:
  0.7 0.7 copy-start.4
  0.7 0.7 copy-start.5
  0.8 0.7 copy-start.6
  0.8 0.7 copy-start.7
  1.4 1.2 %copy-start = (bf16[2,512,512]{2,1,0:T(8,128)(2,1)S(1)}, bf16[2,512,512]{2,1,0:T(8,128)(2,1)}, u32[]{:S(2)}) copy-start(bf16[2,512,512]{2,1,0:T(8,128)(2,1)} %constant.31.clone.hy) | copy-start | bytes 3145732
  2.7 1.0 %copy-start.1 = (f32[3,8,32,128]{3,2,1,0:T(8,128)S(1)}, f32[3,8,32,128]{3,2,1,0:T(8,128)}, u32[]{:S(2)}) copy-start(f32[3,8,32,128]{3,2,1,0:T(8,128)} %p_in.1) | copy-start | bytes 1179652
  3.7 1.0 %copy-start.2 = (bf16[2,320,256]{2,1,0:T(8,128)(2,1)S(1)}, bf16[2,320,256]{2,1,0:T(8,128)(2,1)}, u32[]{:S(2)}) copy-start(bf16[2,320,256]{2,1,0:T(8,128)(2,1)} %constant.30.clone.hx) | copy-start | bytes 983044
  4.6 0.9 %copy-start.3 = (f32[8,32,128]{2,1,0:T(8,128)S(1)}, f32[8,32,128]{2,1,0:T(8,128)}, u32[]{:S(2)}) copy-start(f32[8,32,128]{2,1,0:T(8,128)} %alpha.1) | copy-start | bytes 393220

commit v3 on v2

--- a/solution.py
+++ b/solution.py
@@ -11,7 +11,6 @@
 STEPS = 2
 step_size = 0.05
 MESH = pl.DeviceIdType.MESH
-PAD = 8
 
 
 def cas_table(left, right, length):
@@ -45,22 +44,26 @@
     return dot(left[0], right[0]) + (dot(left[0], right[1]) + dot(left[1], right[0]))
 
 
-def kernel(sizes, p_in, alpha, landau, stiff, perm, inter, lam, hx, hy, p_out, f_out, *scratch):
+def kernel(sizes, p_in, alpha_h, landau, stiff, perm, inter, lam, hx_h, hy_h, p_out, f_out, *scratch):
     L, R, C, nbx, nby, rep, lp, own = sizes
     (p_mid, base, coef, ratio, q, inb, outs, rec_i,
-     row_s, row_r, col_s, col_r, pc_s, pc_r, ssem, rsem) = scratch[:16]
+     row_s, row_r, col_s, col_r, pr_s, pr_r, pc_s, pc_r, ssem, rsem,
+     alpha, hx, hy, local_sem) = scratch[:22]
     wide = is_wide(R, nbx, nby, L)
     if wide:
-        z_in, w_out = scratch[16:]
+        z_in, w_out = scratch[22:]
     else:
-        rec_f, ybuf, phat, u = scratch[16:]
+        rec_f, ybuf, phat, u = scratch[22:]
     thin = R // nby
-    R2 = R + PAD
     bx = lax.axis_index("bx")
     by = lax.axis_index("by")
     group = bx // rep
     part = bx % rep
     scale = 1.0 / (R * nbx * C * nby)
+    loads = [pltpu.make_async_copy(src, dst, local_sem.at[at]) for at, (src, dst) in
+             enumerate(((alpha_h, alpha), (hx_h, hx), (hy_h, hy)))]
+    for load in loads:
+        load.start()
     slots = [0]
     sends = []
 
@@ -124,7 +127,7 @@
             copy.wait_recv()
         table = (hx[0], hx[1])
         for layer in range(lp):
-            outs[n, :, layer] = product(table, halves(inb[n, layer])).reshape(own, R2, C)
+            outs[n, :, layer] = product(table, halves(inb[n, layer])).reshape(own, R, C)
 
     def spread(n, step):
         copies = []
@@ -163,13 +166,13 @@
             values.insert(0, primes[l] + ratio[l] * values[0])
         return values
 
-    def x_finish(n, dst, height):
+    def x_finish(n, dst):
         waits = []
         landing = dst.at[pl.ds(group * lp, lp)]
         for t in range(own):
             local = (group + t) % own
             to = part * own + local
-            src = outs.at[n, local, :, pl.ds(0, height)]
+            src = outs.at[n, local]
             if rep == 1:
                 if t == 0:
                     continue
@@ -198,7 +201,7 @@
 
         def keep():
             for layer in range(lp):
-                dst[group * lp + layer] = outs[n, bx % own, layer, 0:height]
+                dst[group * lp + layer] = outs[n, bx % own, layer]
 
         if rep == 1:
             keep()
@@ -231,7 +234,12 @@
             copies.append(push(row_s.at[step, 0], row_r.at[step, 1], {"bx": (bx + nbx - 1) % nbx}))
             tile, land = col_s.at[step], col_r
         else:
-            pc_s[step] = column_tile([src[l, 0:R] for l in range(L)])
+            for l in range(L):
+                pr_s[step, 0, l:l + 1] = src[l, 0:1]
+                pr_s[step, 1, l:l + 1] = src[l, R - 1:R]
+            copies.append(push(pr_s.at[step, 1], pr_r.at[step, 0], {"bx": (bx + 1) % nbx}))
+            copies.append(push(pr_s.at[step, 0], pr_r.at[step, 1], {"bx": (bx + nbx - 1) % nbx}))
+            pc_s[step] = column_tile([src[l] for l in range(L)])
             tile, land = pc_s.at[step], pc_r
         copies.append(push(tile, land.at[step, 0], {"by": (by + 1) % nby}))
         copies.append(push(tile, land.at[step, 1], {"by": (by + nby - 1) % nby}))
@@ -272,6 +280,9 @@
                 (x_next(along_x, high) - x_prev(along_x, low))
                 + (y_next(along_y, right) - y_prev(along_y, left)) + (above - below))
         copies = x_start(q.at[step], 2 * step)
+        if step == 0:
+            for load in loads:
+                load.wait()
         for l in range(L):
             cells = [src[c, l] for c in range(3)]
             squares = [cell * cell for cell in cells]
@@ -302,39 +313,37 @@
                 w_out[step, j] = full[:, j * C:(j + 1) * C].reshape(L, thin, C)
             copies = collect(n + 1, step)
         else:
-            x_finish(n, rec_f.at[step], R)
+            x_finish(n, rec_f.at[step])
             for l, value in enumerate(solve(y_pass(rec_f.at[step], n), R)):
                 phat[step, l] = value
             u[step] = y_pass(phat.at[step], n + 1).reshape(L, R, C)
             copies = x_start(u.at[step], n + 1)
         x_mix(copies, n + 1)
-        x_finish(n + 1, rec_i.at[step], R2)
+        x_finish(n + 1, rec_i.at[step])
         flanks = flank_start(False, step, rec_i.at[step])
         last = step == STEPS - 1
         target = p_out if last else p_mid
         for l in range(L):
-            phi = rec_i[step, l, 0:R]
-            low = rec_i[step, l, R:R + 1]
-            high = rec_i[step, l, R + 1:R + 2]
-            along_x = -0.5 * (x_next(phi, high) - x_prev(phi, low))
-            above = rec_i[step, l + 1, 0:R] if l + 1 < L else zero
-            below = rec_i[step, l - 1, 0:R] if l else zero
+            above = rec_i[step, l + 1] if l + 1 < L else zero
+            below = rec_i[step, l - 1] if l else zero
             along_z = -0.5 * (above - below)
-            target[0, l] = base[0, l] + step_size * along_x
             target[2, l] = base[2, l] + step_size * along_z
             if last:
-                f_out[0, l] = along_x
                 f_out[2, l] = along_z
         for copy in flanks:
             copy.wait_recv()
         low_phi = pc_r[step, 0]
         high_phi = pc_r[step, 1]
         for l in range(L):
-            phi = rec_i[step, l, 0:R]
+            phi = rec_i[step, l]
+            along_x = -0.5 * (x_next(phi, pr_r[step, 1, l:l + 1])
+                              - x_prev(phi, pr_r[step, 0, l:l + 1]))
             along_y = -0.5 * (y_next(phi, high_phi[:, l:l + 1])
                               - y_prev(phi, low_phi[:, C // 2 + l:C // 2 + l + 1]))
+            target[0, l] = base[0, l] + step_size * along_x
             target[1, l] = base[1, l] + step_size * along_y
             if last:
+                f_out[0, l] = along_x
                 f_out[1, l] = along_y
     for wait in sends:
         wait()
@@ -350,16 +359,14 @@
     lp = max(1, L // nbx)
     own = nbx // rep
     grid_x, grid_y = nbx * R, nby * C
-    R2 = R + PAD
     wide = is_wide(R, nbx, nby, L)
     pool = np if wide else jnp
     make = fixed_table if wide else cas_table
-    line = pool.arange(R2, dtype=jnp.int32)
-    line = pool.where(line < R, line, pool.where(line == R, -1, R))
+    line = pool.arange(R, dtype=jnp.int32)
     owners = pool.arange(own, dtype=jnp.int32)
     if not wide:
         owners = owners + bx % rep * own
-    wanted = ((owners[:, None] * R + line[None, :] + grid_x) % grid_x).reshape(own * R2, 1)
+    wanted = (owners[:, None] * R + line[None, :]).reshape(own * R, 1)
     hx = make(wanted, pool.arange(grid_x, dtype=jnp.int32)[None, :], grid_x)
     every_col = pool.arange(grid_y, dtype=jnp.int32)
     my_rows = bx * R + jnp.arange(R, dtype=jnp.int32)
@@ -374,20 +381,24 @@
     wave_y = jnp.sin(jnp.pi * my_cols.astype(jnp.float32) / grid_y)
     lam = 4.0 * wave_x[:, None] ** 2 + 4.0 * wave_y[None, :] ** 2
     sizes = (L, R, C, nbx, nby, rep, lp, own)
-    n_copies = STEPS * (6 + 2 * (nbx * nby + own if wide else nbx + own + nby))
+    n_copies = STEPS * (8 + 2 * (nbx * nby + own if wide else nbx + own + nby))
     f32 = jnp.float32
     vmem = pl.BlockSpec(memory_space=pltpu.VMEM)
+    hbm = pl.BlockSpec(memory_space=pltpu.HBM)
     smem = pl.BlockSpec(memory_space=pltpu.SMEM)
     S = STEPS
     scratch = [
         pltpu.VMEM((3, L, R, C), f32), pltpu.VMEM((3, L, R, C), f32),
         pltpu.VMEM((L,) + lam.shape, f32), pltpu.VMEM((L,) + lam.shape, f32),
         pltpu.VMEM((S, L, R, C), f32), pltpu.VMEM((2 * S, lp, grid_x, C), f32),
-        pltpu.VMEM((2 * S, own, lp, R2, C), f32), pltpu.VMEM((S, L, R2, C), f32),
+        pltpu.VMEM((2 * S, own, lp, R, C), f32), pltpu.VMEM((S, L, R, C), f32),
         pltpu.VMEM((S, 2, 3 * L, C), f32), pltpu.VMEM((S, 2, 3 * L, C), f32),
         pltpu.VMEM((S, R, C), f32), pltpu.VMEM((S, 2, R, C), f32),
+        pltpu.VMEM((S, 2, L, C), f32), pltpu.VMEM((S, 2, L, C), f32),
         pltpu.VMEM((S, R, C), f32), pltpu.VMEM((S, 2, R, C), f32),
         pltpu.SemaphoreType.DMA((n_copies,)), pltpu.SemaphoreType.DMA((n_copies,)),
+        pltpu.VMEM((L, R, C), f32), pltpu.VMEM(hx.shape, hx.dtype),
+        pltpu.VMEM(hy.shape, hy.dtype), pltpu.SemaphoreType.DMA((3,)),
     ]
     if wide:
         thin = (S, nby, L, R // nby, C)
@@ -401,7 +412,7 @@
     return pl.pallas_call(
         functools.partial(kernel, sizes),
         out_shape=(out, out),
-        in_specs=[vmem, vmem, smem, smem, smem, smem, vmem, vmem, vmem],
+        in_specs=[vmem, hbm, smem, smem, smem, smem, vmem, hbm, hbm],
         out_specs=(vmem, vmem),
         scratch_shapes=scratch,
         compiler_params=pltpu.CompilerParams(

time: 77 us -> 78.9 us (1.025); the launches traced: 75.8 us -> 78.7 us
  Pallas kernels: 68.7 us -> 71.6 us
    pallas_call x1, Pallas kernels: 68.7 us -> 71.6 us  [shards(): pl.pallas_call(functools.partial(kernel, sizes), out_shape=(out, out), in...]
where the time goes in v3:
time: 78.9 us; the launch traced here: 78.7 us
  Pallas kernels  71.6 us (91%)
  local copies, waits for them, and re-layouts  6.17 us (8%)
    pallas_call x1, Pallas kernels, shards(): pl.pallas_call(functools.partial(kernel, sizes), out_shape=(out, out), in...  71.6 us
    unnamed x18, local copies, waits for them, and re-layouts  6.17 us

profile of v3, /device:TPU:0, one launch (start us, length us, event | category | flops | bytes accessed | tf_op | source)
XLA Modules:
  0.0 78.7 jit_solution(9131613235006944307)
XLA Ops:
  0.7 0.0 copy-start.4
  0.7 0.0 copy-start.5
  0.8 0.0 copy-start.6
  0.8 0.0 copy-start.7
  0.8 0.1 broadcast_add_fusion.lam
  0.9 0.6 copy-done.4
  1.4 0.0 copy-done.5
  1.4 0.0 copy-done.6
  1.4 0.0 copy-done.7
  1.4 0.0 copy-start
  1.4 1.2 %copy-done = bf16[2,512,512]{2,1,0:T(8,128)(2,1)S(1)} copy-done((bf16[2,512,512]{2,1,0:T(8,128)(2,1)S(1)}, bf16[2,512,512]{2,1,0:T(8,128)(2,1)}, u32[]{:S(2)}) %copy-start) | copy-done | bytes 1048600
  2.7 0.0 copy-start.1
  2.7 1.0 %copy-done.1 = f32[3,8,32,128]{3,2,1,0:T(8,128)S(1)} copy-done((f32[3,8,32,128]{3,2,1,0:T(8,128)S(1)}, f32[3,8,32,128]{3,2,1,0:T(8,128)}, u32[]{:S(2)}) %copy-start.1) | copy-done | bytes 393240
  3.7 0.0 copy-start.2
  3.7 0.9 %copy-done.2 = bf16[2,256,256]{2,1,0:T(8,128)(2,1)S(1)} copy-done((bf16[2,256,256]{2,1,0:T(8,128)(2,1)S(1)}, bf16[2,256,256]{2,1,0:T(8,128)(2,1)}, u32[]{:S(2)}) %copy-start.2) | copy-done | bytes 262168
  4.6 0.0 copy-start.3
  4.6 0.9 %copy-done.3 = f32[8,32,128]{2,1,0:T(8,128)S(1)} copy-done((f32[8,32,128]{2,1,0:T(8,128)S(1)}, f32[8,32,128]{2,1,0:T(8,128)}, u32[]{:S(2)}) %copy-start.3) | copy-done | bytes 131096
  5.5 71.6 %shard_map.95 = (f32[3,8,32,128]{3,2,1,0:T(8,128)S(1)}, f32[3,8,32,128]{3,2,1,0:T(8,128)S(1)}) custom-call(f32[3,8,32,128]{3,2,1,0:T(8,128)S(1)} %copy-done.1, f32[8,32,128]{2,1,0:T(8,128)S(1)} %copy-done.3, f32[3,8]{1,0:T(4,128)S(1)} %copy-done.4, f32[8]{0:T(128)S(1)} %copy-done.5, f32[8]{0:T(128)S(1)} %copy-done.6, f32[9]{0:T(128)S(1)} %copy-done.7, ...), custom_call_target="tpu_custom_call" | custom-call | tf_op jit(solution)/shard_map/pallas_call | solution.py:412
  77.2 0.7 copy.12
  77.9 0.7 copy.13
  (2 shorter events, 0.1 us)
Async XLA Ops:
  0.7 0.7 copy-start.4
  0.7 0.7 copy-start.5
  0.8 0.7 copy-start.6
  0.8 0.7 copy-start.7
  1.4 1.2 %copy-start = (bf16[2,512,512]{2,1,0:T(8,128)(2,1)S(1)}, bf16[2,512,512]{2,1,0:T(8,128)(2,1)}, u32[]{:S(2)}) copy-start(bf16[2,512,512]{2,1,0:T(8,128)(2,1)} %constant.31.clone.hy_h) | copy-start | bytes 3145732
  2.7 1.0 %copy-start.1 = (f32[3,8,32,128]{3,2,1,0:T(8,128)S(1)}, f32[3,8,32,128]{3,2,1,0:T(8,128)}, u32[]{:S(2)}) copy-start(f32[3,8,32,128]{3,2,1,0:T(8,128)} %p_in.1) | copy-start | bytes 1179652
  3.7 0.9 %copy-start.2 = (bf16[2,256,256]{2,1,0:T(8,128)(2,1)S(1)}, bf16[2,256,256]{2,1,0:T(8,128)(2,1)}, u32[]{:S(2)}) copy-start(bf16[2,256,256]{2,1,0:T(8,128)(2,1)} %constant.30.clone.hx_h) | copy-start | bytes 786436
  4.6 0.9 %copy-start.3 = (f32[8,32,128]{2,1,0:T(8,128)S(1)}, f32[8,32,128]{2,1,0:T(8,128)}, u32[]{:S(2)}) copy-start(f32[8,32,128]{2,1,0:T(8,128)} %alpha_h.1) | copy-start | bytes 393220

commit v4 on v2

--- a/solution.py
+++ b/solution.py
@@ -45,15 +45,16 @@
     return dot(left[0], right[0]) + (dot(left[0], right[1]) + dot(left[1], right[0]))
 
 
-def kernel(sizes, p_in, alpha, landau, stiff, perm, inter, lam, hx, hy, p_out, f_out, *scratch):
+def kernel(sizes, p_in, alpha_h, landau, stiff, perm, inter, lam, hx_h, hy_h, p_out, f_out, *scratch):
     L, R, C, nbx, nby, rep, lp, own = sizes
     (p_mid, base, coef, ratio, q, inb, outs, rec_i,
-     row_s, row_r, col_s, col_r, pc_s, pc_r, ssem, rsem) = scratch[:16]
+     row_s, row_r, col_s, col_r, pc_s, pc_r, ssem, rsem,
+     alpha, hx, hy, local_sem) = scratch[:20]
     wide = is_wide(R, nbx, nby, L)
     if wide:
-        z_in, w_out = scratch[16:]
+        z_in, w_out = scratch[20:]
     else:
-        rec_f, ybuf, phat, u = scratch[16:]
+        rec_f, ybuf, phat, u = scratch[20:]
     thin = R // nby
     R2 = R + PAD
     bx = lax.axis_index("bx")
@@ -61,6 +62,10 @@
     group = bx // rep
     part = bx % rep
     scale = 1.0 / (R * nbx * C * nby)
+    loads = [pltpu.make_async_copy(src, dst, local_sem.at[at]) for at, (src, dst) in
+             enumerate(((alpha_h, alpha), (hx_h, hx), (hy_h, hy)))]
+    for load in loads:
+        load.start()
     slots = [0]
     sends = []
 
@@ -272,6 +277,9 @@
                 (x_next(along_x, high) - x_prev(along_x, low))
                 + (y_next(along_y, right) - y_prev(along_y, left)) + (above - below))
         copies = x_start(q.at[step], 2 * step)
+        if step == 0:
+            for load in loads:
+                load.wait()
         for l in range(L):
             cells = [src[c, l] for c in range(3)]
             squares = [cell * cell for cell in cells]
@@ -377,6 +385,7 @@
     n_copies = STEPS * (6 + 2 * (nbx * nby + own if wide else nbx + own + nby))
     f32 = jnp.float32
     vmem = pl.BlockSpec(memory_space=pltpu.VMEM)
+    hbm = pl.BlockSpec(memory_space=pltpu.HBM)
     smem = pl.BlockSpec(memory_space=pltpu.SMEM)
     S = STEPS
     scratch = [
@@ -388,6 +397,8 @@
         pltpu.VMEM((S, R, C), f32), pltpu.VMEM((S, 2, R, C), f32),
         pltpu.VMEM((S, R, C), f32), pltpu.VMEM((S, 2, R, C), f32),
         pltpu.SemaphoreType.DMA((n_copies,)), pltpu.SemaphoreType.DMA((n_copies,)),
+        pltpu.VMEM((L, R, C), f32), pltpu.VMEM(hx.shape, hx.dtype),
+        pltpu.VMEM(hy.shape, hy.dtype), pltpu.SemaphoreType.DMA((3,)),
     ]
     if wide:
         thin = (S, nby, L, R // nby, C)
@@ -401,11 +412,11 @@
     return pl.pallas_call(
         functools.partial(kernel, sizes),
         out_shape=(out, out),
-        in_specs=[vmem, vmem, smem, smem, smem, smem, vmem, vmem, vmem],
+        in_specs=[vmem, hbm, smem, smem, smem, smem, vmem, hbm, hbm],
         out_specs=(vmem, vmem),
         scratch_shapes=scratch,
         compiler_params=pltpu.CompilerParams(
-            collective_id=0, has_side_effects=True, vmem_limit_bytes=48 * 1024 * 1024),
+            collective_id=0, has_side_effects=True, vmem_limit_bytes=65 * 1000 * 1000),
     )(polarization, alpha_field, landau, stiffness, permittivity, interfaces, lam, hx, hy)
 
 

time: 77 us -> 75.2 us (0.977)
  local copies, waits for them, and re-layouts: 6.19 us -> 2.57 us
  Pallas kernels: 68.7 us -> 70 us
    unnamed x18 -> x4, local copies, waits for them, and re-layouts: 6.19 us -> 2.57 us
    pallas_call x1, Pallas kernels: 68.7 us -> 70 us  [shards(): pl.pallas_call(functools.partial(kernel, sizes), out_shape=(out, out), in...]
where the time goes in v4:
time: 75.2 us; the launch traced here: 74 us
  Pallas kernels  70 us (93%)
  local copies, waits for them, and re-layouts  2.57 us (3%)
  other arithmetic  0.77 us (1%)
    pallas_call x1, Pallas kernels, shards(): pl.pallas_call(functools.partial(kernel, sizes), out_shape=(out, out), in...  70 us
    unnamed x4, local copies, waits for them, and re-layouts  2.57 us

profile of v4, /device:TPU:0, one launch (start us, length us, event | category | flops | bytes accessed | tf_op | source)
XLA Modules:
  0.0 74.0 jit_solution(17915008343972579319)
XLA Ops:
  0.7 0.7 broadcast_add_fusion.lam
  1.4 70.0 %shard_map.95 = (f32[3,8,32,128]{3,2,1,0:T(8,128)}, f32[3,8,32,128]{3,2,1,0:T(8,128)}) custom-call(f32[3,8,32,128]{3,2,1,0:T(8,128)} %p_in.1, f32[8,32,128]{2,1,0:T(8,128)} %alpha_h.1, f32[3,8]{1,0:T(4,128)} %landau.1, f32[8]{0:T(128)} %stiff.1, f32[8]{0:T(128)} %perm.1, f32[9]{0:T(128)} %inter.1, f32[8,512]{1,0:T(8,128)} %broadcast_add_fusion.lam, ...), custom_call_target="tpu_custom_call" | custom-call | tf_op jit(solution)/shard_map/pallas_call | solution.py:412
  71.5 0.0 copy-start
  71.5 1.8 %copy.12 = f32[3,8,32,128]{3,2,1,0:T(8,128)} copy(f32[3,8,32,128]{3,2,1,0:T(8,128)} %get-tuple-element.4) | data formatting | bytes 786432
  73.3 0.0 copy-done
  73.3 0.7 %copy.13 = f32[3,8,32,128]{3,2,1,0:T(8,128)} copy(f32[3,8,32,128]{3,2,1,0:T(8,128)S(1)} %copy-done) | data formatting | bytes 786432
  (2 shorter events, 0.1 us)
Async XLA Ops:
  71.5 1.8 %copy-start = (f32[3,8,32,128]{3,2,1,0:T(8,128)S(1)}, f32[3,8,32,128]{3,2,1,0:T(8,128)}, u32[]{:S(2)}) copy-start(f32[3,8,32,128]{3,2,1,0:T(8,128)} %get-tuple-element.5) | copy-start | bytes 1179652
